TPU v7x, 32 devices: a whole 2x2x4 slice. The times are simulated.
32 devices in a mesh: seq: 8 (over y, x, core), exp: 4 (over z).
Axes of the slice: x: 2, y: 2, z: 4, core: 2. Of those that a mesh axis runs over, the one named last changes fastest.
Arguments:
- queries: bfloat16 [1024, 4096], P('seq', 'exp'), may hold values from -135 to 135
- attn_keys: bfloat16 [1024, 512], P('seq', 'exp'), may hold values from -4.5 to 4.5
- attn_values: bfloat16 [1024, 512], P('seq', 'exp'), may hold values from -6 to 6
- sink_logits: float32 [64], P('exp'), may hold values from -1 to 3
- out_proj: bfloat16 [4096, 2880], P('exp'), may hold values from -0.09375 to 0.09375
- residual: bfloat16 [1024, 2880], P('seq', 'exp'), may hold values from -6 to 6
- norm_gain: float32 [2880], replicated, may hold values from 0.5 to 1.5
- doc_start: int32 [1024], P('seq'), may hold values from 0 to 1023, as said below
- expert_ids: int32 [1024, 4], P('seq'), may hold values from 0 to 7, all different within a row; in each aligned block of 128 rows (0 to 127, 128 to 255, ...) at most 128 rows name the same one
- route_scores: float32 [1024, 4], P('seq'), may hold values from 0.2 to 1
- w_gate_up: bfloat16 [8, 2, 2880, 2880], P('seq', None, None, 'exp'), may hold values from -0.109375 to 0.109375
- w_down: bfloat16 [8, 2880, 2880], P('seq', 'exp'), may hold values from -0.109375 to 0.109375
- control: float32 [2880], replicated, may hold values from 0 to 1
Outputs:
- grad_gate_up: bfloat16 [8, 2, 2880, 2880], P('seq', None, None, 'exp')
Inputs may be any that keep to these rules, and one draw needn't show every extreme that they name: `expert_ids`: each row names 4 different experts; among the 128 rows of one index of seq no expert is named by more than 128 rows, a bound that some block reaches. doc_start of a position is the first position of its document: never above the position itself, never falling along the pack, equal within a document; position 0 starts a document, and the last position of the pack is a document of its own.
All inputs are finite; a program needn't handle non-finite values.
Results may differ from a plain program's by a relative error of at most 0.0075.
Values may be sent and summed in bfloat16 or wider, within the bound.
A program may use at most 128 MiB of HBM per device.

v0:
```python
import jax
import jax.numpy as jnp
from jax import lax
from jax.sharding import PartitionSpec as P

D = 2880
HEAD_DIM = 64
WINDOW = 128
TOPK = 4


GLU_ALPHA = 1.702
STEER = 6.5
EPSILON = 1e-05
MASKED = -1e30


def passed_along(block, axis, distance):
    devices = range(lax.axis_size(axis))
    route = [(i - distance, i) for i in devices if i - distance in devices]
    return lax.ppermute(block, axis, route)


def attend(queries, attn_keys, attn_values, sink_logits, doc_start):
    seg_len = queries.shape[0]
    heads_here = queries.shape[1] // HEAD_DIM
    kv_here = attn_keys.shape[1] // HEAD_DIM
    group_size = heads_here // kv_here
    both_rims = passed_along(jnp.stack([attn_keys, attn_values]), "seq", 1)
    keys_all = jnp.concatenate([both_rims[0], attn_keys], axis=0).reshape(
        WINDOW + seg_len, kv_here, HEAD_DIM
    )
    values_all = jnp.concatenate([both_rims[1], attn_values], axis=0).reshape(
        WINDOW + seg_len, kv_here, HEAD_DIM
    )
    offset = lax.axis_index("seq") * seg_len
    query_pos = offset + jnp.arange(seg_len, dtype=jnp.int32)
    key_pos = offset - WINDOW + jnp.arange(WINDOW + seg_len, dtype=jnp.int32)
    allowed = (
        (key_pos[None, :] <= query_pos[:, None])
        & (key_pos[None, :] > query_pos[:, None] - WINDOW)
        & (key_pos[None, :] >= doc_start[:, None])
    )
    grouped = queries.reshape(seg_len, kv_here, group_size, HEAD_DIM)
    scores = jnp.einsum(
        "qcgd,kcd->cgqk", grouped, keys_all, preferred_element_type=jnp.float32
    ) * HEAD_DIM ** (-0.5)
    masked_scores = jnp.where(allowed[None, None], scores, MASKED)
    sink_grid = sink_logits.reshape(kv_here, group_size, 1, 1)
    row_top = jnp.maximum(jnp.max(masked_scores, axis=-1, keepdims=True), sink_grid)
    expo_scores = jnp.where(allowed[None, None], jnp.exp(masked_scores - row_top), 0.0)
    denominator = jnp.sum(expo_scores, axis=-1, keepdims=True) + jnp.exp(sink_grid - row_top)
    attn_weights = (expo_scores / denominator).astype(jnp.bfloat16)
    mixed_heads = jnp.einsum(
        "cgqk,kcd->qcgd", attn_weights, values_all, preferred_element_type=jnp.float32
    )
    return mixed_heads.astype(jnp.bfloat16).reshape(seg_len, heads_here * HEAD_DIM)


def slice_total(partial_value):
    return lax.psum(partial_value, "exp")


def to_owners(buffer):
    return lax.all_to_all(buffer, "seq", split_axis=0, concat_axis=0, tiled=True)


def gather_outputs(out_part, flat_ids, slot_rank, capacity):
    width = out_part.shape[-1]
    returned = lax.all_to_all(out_part, "seq", split_axis=0, concat_axis=0, tiled=True).reshape(
        -1, width
    )
    return returned[flat_ids * capacity + slot_rank].astype(jnp.float32)


def shards(
    queries,
    attn_keys,
    attn_values,
    sink_logits,
    out_proj,
    residual,
    norm_gain,
    doc_start,
    expert_ids,
    route_scores,
    w_gate_up,
    w_down,
    control,
):
    n_seq = lax.axis_size("seq")
    seg_len = queries.shape[0]
    capacity = 2 * TOPK * seg_len // n_seq
    block_index = lax.axis_index("exp")
    heads_out = attend(queries, attn_keys, attn_values, sink_logits, doc_start)
    partial_value = jnp.dot(heads_out, out_proj, preferred_element_type=jnp.float32)
    column_width = residual.shape[1]
    own_columns = lax.dynamic_slice_in_dim(
        partial_value, block_index * column_width, column_width, 1
    ) + residual.astype(jnp.float32)
    partial_value = lax.dynamic_update_slice_in_dim(
        partial_value, own_columns, block_index * column_width, 1
    )
    mixed = slice_total(partial_value)
    normed = (
        mixed * lax.rsqrt(jnp.mean(mixed * mixed, axis=-1, keepdims=True) + EPSILON) * norm_gain
    ).astype(jnp.bfloat16)
    route_gates = route_scores / jnp.sum(route_scores, axis=-1, keepdims=True)
    flat_ids = expert_ids.reshape(-1)
    onehot = (flat_ids[:, None] == jnp.arange(n_seq, dtype=jnp.int32)[None, :]).astype(jnp.int32)
    slot_rank = jnp.sum((jnp.cumsum(onehot, axis=0) - 1) * onehot, axis=1)
    slot_index = flat_ids * capacity + slot_rank
    owner_row = (
        jnp.zeros((n_seq * capacity,), jnp.int32)
        .at[slot_index]
        .set(jnp.arange(seg_len * TOPK, dtype=jnp.int32))
    )
    filled = (
        jnp.zeros((n_seq * capacity,), jnp.bfloat16)
        .at[slot_index]
        .set(jnp.ones((seg_len * TOPK,), jnp.bfloat16))
    )
    sent_rows = (normed[owner_row // TOPK] * filled[:, None]).reshape(n_seq, capacity, D)
    rows_flat = to_owners(sent_rows).reshape(-1, D)
    gate_slice = w_gate_up[0, 0]
    up_slice = w_gate_up[0, 1]
    down_slice = w_down[0]
    gate_value = jnp.dot(rows_flat, gate_slice, preferred_element_type=jnp.float32)
    up_value = jnp.dot(rows_flat, up_slice, preferred_element_type=jnp.float32)
    squashed = jax.nn.sigmoid(GLU_ALPHA * gate_value)
    glu_value = gate_value * squashed
    hidden = ((up_value + 1.0) * glu_value).astype(jnp.bfloat16)
    out_part = (
        jnp.dot(hidden, down_slice, preferred_element_type=jnp.float32)
        .astype(jnp.bfloat16)
        .reshape(n_seq, capacity, D)
    )
    picked = gather_outputs(out_part, flat_ids, slot_rank, capacity).reshape(seg_len, TOPK, D)
    moe_out = slice_total(jnp.sum(route_gates[:, :, None] * picked, axis=1))
    target = STEER * control / jnp.sqrt(jnp.sum(control * control))
    residual_error = mixed + moe_out - target[None, :]
    d_out = (
        (route_gates[:, :, None] * residual_error[:, None, :])
        .astype(jnp.bfloat16)
        .reshape(seg_len * TOPK, D)
    )
    sent_back = (d_out[owner_row] * filled[:, None]).reshape(n_seq, capacity, D)
    grads_in = to_owners(sent_back).reshape(-1, D)
    d_hidden = lax.dot_general(
        grads_in, down_slice, (((1,), (1,)), ((), ())), preferred_element_type=jnp.float32
    )
    d_gate = (
        d_hidden
        * (up_value + 1.0)
        * (squashed + GLU_ALPHA * gate_value * squashed * (1.0 - squashed))
    ).astype(jnp.bfloat16)
    d_up = (d_hidden * glu_value).astype(jnp.bfloat16)
    grad_gate = lax.dot_general(
        rows_flat, d_gate, (((0,), (0,)), ((), ())), preferred_element_type=jnp.float32
    )
    grad_up = lax.dot_general(
        rows_flat, d_up, (((0,), (0,)), ((), ())), preferred_element_type=jnp.float32
    )
    return jnp.stack([grad_gate, grad_up])[None].astype(jnp.bfloat16)


def solution(mesh):
    return jax.shard_map(
        shards,
        mesh=mesh,
        in_specs=(
            P("seq", "exp"),
            P("seq", "exp"),
            P("seq", "exp"),
            P("exp"),
            P("exp", None),
            P("seq", "exp"),
            P(),
            P("seq"),
            P("seq", None),
            P("seq", None),
            P("seq", None, None, "exp"),
            P("seq", "exp", None),
            P(),
        ),
        out_specs=P("seq", None, None, "exp"),
        check_vma=False,
    )
```

profile of v0, /device:TPU:0, one launch (start us, length us, event | category | flops | bytes accessed | tf_op | source)
XLA Modules:
  0.0 538.8 jit_solution(5574979194936990726)
XLA Ops:
  6.5 0.8 pad_maximum_fusion.1
  7.3 2.4 collective-permute-start
  9.7 0.8 compare_and_fusion
  10.5 0.9 copy.59
  11.4 0.9 copy.57
  12.3 1.1 copy.60
  13.4 0.7 max.18
  14.8 1.2 copy-done.2
  16.8 2.5 convolution_convert_fusion.2
  19.8 1.7 fusion.46
  21.6 1.1 copy-done.1
  23.0 1.1 reduce-window.6
  24.8 2.4 scatter_custom_fusion
  27.2 3.8 scatter_custom_fusion.1
  31.0 60.1 %all-reduce.3.cloned.1.call-done = f32[128,2880]{0,1:T(8,128)} async-done(((f32[128,2880]{0,1:T(8,128)}), f32[128,2880]{0,1:T(8,128)}) %all-reduce.3.cloned.1.call-update) | async-done | bytes 1474576 | tf_op jit(solution)/shard_map/psum | solution.py:61
  91.1 1.8 multiply_reduce_fusion.1
  92.9 1.8 multiply_convert_fusion.7
  95.1 6.5 %gather_fusion = bf16[1024,2880]{1,0:T(8,128)(2,1)} fusion(bf16[128,2880]{1,0:T(8,128)(2,1)S(1)} %copy.65, s32[1024]{0:T(1024)S(1)} %get-tuple-element.8), kind=kCustom, calls=%fused_computation | custom fusion | bytes 11800576 | tf_op jit(solution)/shard_map/gather | solution.py:123
  101.6 8.4 %copy.66 = bf16[8,128,2880]{1,2,0:T(8,128)(2,1)} copy(bf16[8,128,2880]{2,1,0:T(8,128)(2,1)} %bitcast.76) | data formatting | bytes 11796480 | tf_op jit(solution)/shard_map/gather | solution.py:123
  110.0 3.1 broadcast_multiply_fusion.1
  113.0 71.3 %all_to_all.15 = bf16[8,128,2880]{1,2,0:T(8,128)(2,1)} all-to-all(bf16[8,128,2880]{1,2,0:T(8,128)(2,1)S(1)} %broadcast_multiply_fusion.1), channel_id=1, replica_groups=mesh['seq'=8,'exp'=4] {'seq'}, dimensions={0} | all-to-all | bytes 11796480 | tf_op jit(solution)/shard_map/all_to_all | solution.py:65
  184.4 8.5 %copy.67 = bf16[8,128,2880]{2,1,0:T(8,128)(2,1)} copy(bf16[8,128,2880]{1,2,0:T(8,128)(2,1)} %all_to_all.15) | data formatting | bytes 11796480 | tf_op jit(solution)/shard_map/all_to_all | solution.py:65
  192.8 10.5 %fusion.5 = f32[1024,720]{0,1:T(8,128)} fusion(bf16[1024,2880]{1,0:T(8,128)(2,1)} %bitcast.81, bf16[1,2,2880,720]{2,3,1,0:T(8,128)(2,1)} %param.23), kind=kOutput, calls=%fused_computation.17 | convolution fusion | flops 4246732800 | bytes 13217792 | tf_op jit(solution)/shard_map/dot_general | solution.py:128
  203.3 6.4 %fusion.7 = f32[1024,720]{0,1:T(8,128)} fusion(bf16[1024,2880]{1,0:T(8,128)(2,1)S(1)} %bitcast.82, bf16[1,2,2880,720]{2,3,1,0:T(8,128)(2,1)S(1)} %bitcast.103), kind=kOutput, calls=%fused_computation.19 | convolution fusion | flops 4246732800 | bytes 13217792 | tf_op jit(solution)/shard_map/dot_general | solution.py:129
  209.7 8.9 %convert_bitcast_fusion = bf16[360,8,8,128]{3,2,1,0:T(8,128)(2,1)S(1)} fusion(bf16[1,720,2880]{2,1,0:T(8,128)(2,1)} %param.24, f32[1024,720]{0,1:T(8,128)} %fusion.7, f32[1024,720]{0,1:T(8,128)} %fusion.5), kind=kOutput, calls=%fused_computation.9 | convolution fusion | flops 4255580160 | bytes 15943680 | tf_op jit(solution)/shard_map/dot_general | solution.py:134
  218.6 3.6 copy.81
  222.2 4.8 all-to-all-start.1
  227.4 67.0 %all-to-all-done.1 = bf16[8,128,2880]{1,2,0:T(8,128)(2,1)} async-done(((bf16[8,128,2880]{1,2,0:T(8,128)(2,1)}), bf16[8,128,2880]{1,2,0:T(8,128)(2,1)}, u32[]{:S(2)}, u32[]{:S(2)}) %all-to-all-start.1) | async-done | bytes 5898272 | tf_op jit(solution)/shard_map/all_to_all | solution.py:70
  294.4 8.4 %copy.71 = bf16[8,128,2880]{2,1,0:T(8,128)(2,1)} copy(bf16[8,128,2880]{1,2,0:T(8,128)(2,1)} %all-to-all-done.1) | data formatting | bytes 11796480 | tf_op jit(solution)/shard_map/all_to_all | solution.py:70
  302.7 9.3 %gather_fusion.1 = bf16[512,2880]{1,0:T(8,128)(2,1)S(1)} fusion(bf16[1024,2880]{1,0:T(8,128)(2,1)} %bitcast.75, s32[1024]{0:T(1024)S(1)} %pad_clamp_fusion), kind=kCustom, calls=%fused_computation.1 | custom fusion | bytes 5900288 | tf_op jit(solution)/shard_map/gather | solution.py:73
  312.1 3.7 reshape.262
  315.7 7.0 %multiply_reduce_fusion = f32[128,2880]{1,0:T(8,128)S(1)} fusion(f32[128,4,2880]{2,1,0:T(4,128)} %reshape.262, f32[128,4]{1,0:T(8,128)S(1)} %copy.68), kind=kLoop, calls=%fused_computation.7 | loop fusion | flops 2580480 | bytes 7374848 | tf_op jit(solution)/shard_map/reduce_sum | solution.py:139
  322.8 1.6 copy.72
  324.5 0.6 multiply_reduce_fusion.2
  325.7 62.0 %all-reduce.5.cloned.1.call-done = f32[128,2880]{0,1:T(8,128)} async-done(((f32[128,2880]{0,1:T(8,128)}), f32[128,2880]{0,1:T(8,128)}) %all-reduce.5.cloned.1.call-update) | async-done | bytes 1474576 | tf_op jit(solution)/shard_map/psum | solution.py:61
  387.7 1.8 add_subtract_fusion
  390.0 3.6 mul.156
  393.7 7.9 %mul.157 = f32[512,2880]{1,0:T(8,128)} reshape(f32[128,4,2880]{2,1,0:T(4,128)} %mul.156) | data formatting | bytes 11796480 | tf_op jit(solution)/shard_map/mul | solution.py:143
  401.6 3.3 multiply_convert_fusion
  404.9 6.6 %gather_fusion.2 = bf16[1024,2880]{1,0:T(8,128)(2,1)} fusion(bf16[512,2880]{1,0:T(8,128)(2,1)S(1)} %multiply_convert_fusion, s32[1024]{0:T(1024)S(1)} %get-tuple-element.7), kind=kCustom, calls=%fused_computation.2 | custom fusion | bytes 11800576 | tf_op jit(solution)/shard_map/gather | solution.py:147
  411.5 8.4 %copy.74 = bf16[8,128,2880]{1,2,0:T(8,128)(2,1)} copy(bf16[8,128,2880]{2,1,0:T(8,128)(2,1)} %bitcast.77) | data formatting | bytes 11796480 | tf_op jit(solution)/shard_map/gather | solution.py:147
  419.9 3.1 broadcast_multiply_fusion
  423.0 70.9 %all_to_all.16 = bf16[8,128,2880]{1,2,0:T(8,128)(2,1)} all-to-all(bf16[8,128,2880]{1,2,0:T(8,128)(2,1)S(1)} %broadcast_multiply_fusion), channel_id=1, replica_groups=mesh['seq'=8,'exp'=4] {'seq'}, dimensions={0} | all-to-all | bytes 11796480 | tf_op jit(solution)/shard_map/all_to_all | solution.py:65
  493.8 8.6 %copy.75 = bf16[8,128,2880]{2,1,0:T(8,128)(2,1)} copy(bf16[8,128,2880]{1,2,0:T(8,128)(2,1)} %all_to_all.16) | data formatting | bytes 11796480 | tf_op jit(solution)/shard_map/all_to_all | solution.py:65
  502.4 8.2 %fusion.2 = f32[1024,720]{0,1:T(8,128)S(1)} fusion(bf16[1024,2880]{1,0:T(8,128)(2,1)} %bitcast.87, bf16[1,720,2880]{2,1,0:T(8,128)(2,1)} %param.24), kind=kOutput, calls=%fused_computation.14 | convolution fusion | flops 4246732800 | bytes 12994560 | tf_op jit(solution)/shard_map/dot_general | solution.py:149
  510.7 6.9 %fusion = bf16[1,1,2880,720]{2,3,1,0:T(8,128)(2,1)} fusion(bf16[1024,2880]{1,0:T(8,128)(2,1)S(1)} %bitcast.85, f32[1024,720]{0,1:T(8,128)S(1)} %fusion.2, f32[1024,720]{0,1:T(8,128)S(1)} %copy-done.9, f32[1024,720]{0,1:T(8,128)S(1)} %copy-done.10), kind=kOutput, calls=%fused_computation.12 | convolution fusion | flops 4257653760 | bytes 18892800 | tf_op jit(solution)/shard_map/dot_general | solution.py:158
  517.6 6.3 %fusion.1 = bf16[1,1,2880,720]{2,3,1,0:T(8,128)(2,1)} fusion(bf16[1024,2880]{1,0:T(8,128)(2,1)S(1)} %bitcast.86, f32[1024,720]{0,1:T(8,128)S(1)} %fusion.2, f32[1024,720]{0,1:T(8,128)S(1)} %copy-done.9), kind=kOutput, calls=%fused_computation.13 | convolution fusion | flops 4253967360 | bytes 15943680 | tf_op jit(solution)/shard_map/dot_general | solution.py:161
  523.9 7.8 %pad_maximum_fusion = bf16[1,2,2880,720]{2,3,1,0:T(8,128)(2,1)} fusion(bf16[1,1,2880,720]{2,3,1,0:T(8,128)(2,1)} %fusion.1, bf16[1,1,2880,720]{2,3,1,0:T(8,128)(2,1)} %fusion), kind=kLoop, calls=%fused_computation.5 | loop fusion | flops 4147200 | bytes 16588800 | tf_op jit(solution)/shard_map/stack | solution.py:164
  (76 shorter events, 4.3 us)
Async XLA Ops:
  6.5 84.6 %all-reduce.3.cloned.1.call-start = ((), (), s32[]{:S(2)}) async-start(), calls=%async_computation.3 | async-start | bytes 2949120 | tf_op jit(solution)/shard_map/psum | solution.py:61
  7.3 6.8 %collective-permute-start = (bf16[2,128,128]{2,1,0:T(8,128)(2,1)S(1)}, bf16[2,128,128]{2,1,0:T(8,128)(2,1)S(1)}, u32[]{:S(2)}, u32[]{:S(2)}) collective-permute-start(bf16[2,128,128]{2,1,0:T(8,128)(2,1)S(1)} %pad_maximum_fusion.1), channel_id=1, source_target_pairs={{0,4},{4,8},{8,12},{12,16},{16,20},{20,24},{24,28},{1,5},{5,9},{9,... | collective-permute-start | bytes 196616 | tf_op jit(solution)/shard_map/ppermute | solution.py:21
  14.8 1.3 copy-start.2
  16.1 3.2 slice-start
  16.8 3.0 slice-start.1
  19.8 1.7 copy-start.4
  19.8 2.9 copy-start.7
  21.5 71.4 %copy-start.6 = (f32[2880]{0:T(1024)S(1)}, f32[2880]{0:T(1024)}, u32[]{:S(2)}) copy-start(f32[2880]{0:T(1024)} %param.19) | copy-start | bytes 34564
  21.5 1.1 copy-start.1
  184.4 19.0 %slice-start.4 = ((s8[8478720]{0:T(1024)(128)(4,1)}), s8[90112]{0:T(1024)(128)(4,1)S(1)}, s32[]{:S(2)}) async-start(s8[8478720]{0:T(1024)(128)(4,1)} %bitcast.102), calls=%async_computation.9 | async-start | bytes 180224
  192.8 10.5 %copy-start.3 = (bf16[8,128,2880]{2,1,0:T(8,128)(2,1)S(1)}, bf16[8,128,2880]{2,1,0:T(8,128)(2,1)}, u32[]{:S(2)}) copy-start(bf16[8,128,2880]{2,1,0:T(8,128)(2,1)} %copy.67) | copy-start | bytes 17694724
  192.8 10.5 %slice-start.5 = ((s8[8478720]{0:T(1024)(128)(4,1)}), s8[4194304]{0:T(1024)(128)(4,1)S(1)}, s32[]{:S(2)}) async-start(s8[8478720]{0:T(1024)(128)(4,1)} %bitcast.102), calls=%async_computation.10 | async-start | bytes 8388608
  192.8 10.5 %slice-start.6 = ((s8[8478720]{0:T(1024)(128)(4,1)}), s8[4194304]{0:T(1024)(128)(4,1)S(1)}, s32[]{:S(2)}) async-start(s8[8478720]{0:T(1024)(128)(4,1)} %bitcast.102), calls=%async_computation.11 | async-start | bytes 8388608
  222.2 5.1 copy-start.8
  222.2 72.2 %all-to-all-start.1 = ((bf16[8,128,2880]{1,2,0:T(8,128)(2,1)}), bf16[8,128,2880]{1,2,0:T(8,128)(2,1)}, u32[]{:S(2)}, u32[]{:S(2)}) async-start(bf16[8,128,2880]{1,2,0:T(8,128)(2,1)} %bitcast.78), calls=%async_computation.1 | async-start | bytes 11796480 | tf_op jit(solution)/shard_map/all_to_all | solution.py:70
  227.0 160.7 %all-reduce.5.cloned.1.call-start = ((), (), s32[]{:S(2)}) async-start(), calls=%async_computation.4 | async-start | bytes 2949120 | tf_op jit(solution)/shard_map/psum | solution.py:61
  322.7 1.8 copy-start.5
  322.7 65.0 %copy-start = (f32[128,2880]{0,1:T(8,128)S(1)}, f32[128,2880]{0,1:T(8,128)}, u32[]{:S(2)}) copy-start(f32[128,2880]{0,1:T(8,128)} %all-reduce.3.cloned.1.call-done) | copy-start | bytes 4423684
  493.8 16.9 %slice-start.2 = ((s8[6029312]{0:T(1024)(128)(4,1)}), s8[1835008]{0:T(1024)(128)(4,1)S(1)}, s32[]{:S(2)}) async-start(s8[6029312]{0:T(1024)(128)(4,1)} %bitcast.83), calls=%async_computation.7 | async-start | bytes 3670016
  502.4 8.3 %slice-start.3 = ((s8[6029312]{0:T(1024)(128)(4,1)}), s8[4194304]{0:T(1024)(128)(4,1)S(1)}, s32[]{:S(2)}) async-start(s8[6029312]{0:T(1024)(128)(4,1)} %bitcast.83), calls=%async_computation.8 | async-start | bytes 8388608
  502.4 8.3 %copy-start.9 = (f32[1024,720]{0,1:T(8,128)S(1)}, f32[1024,720]{0,1:T(8,128)}, u32[]{:S(2)}) copy-start(f32[1024,720]{0,1:T(8,128)} %fusion.5) | copy-start | bytes 8847364
  502.4 8.3 %copy-start.10 = (f32[1024,720]{0,1:T(8,128)S(1)}, f32[1024,720]{0,1:T(8,128)}, u32[]{:S(2)}) copy-start(f32[1024,720]{0,1:T(8,128)} %fusion.7) | copy-start | bytes 8847364
Sparse Core Ops, SparseCore 0:
  22.8 68.2 all-reduce.2
  324.5 63.1 all-reduce.4
where the time goes:
time: 549 us; the launch traced here: 539 us
  waiting for transfers between devices  189 us (34%)
  blocking collectives  142 us (26%)
  local copies, waits for them, and re-layouts  99.9 us (18%)
  matrix products  51.8 us (9%)
  other arithmetic  33.8 us (6%)
  between operations  14.6 us (3%)
  starting transfers between devices  7.44 us (1%)
    all_to_all x2, blocking collectives, to_owners(): lax.all_to_all(buffer, 'seq', split_axis=0, concat_axis=0, tiled=True)  142 us
    psum x2, waiting for transfers between devices, slice_total(): return lax.psum(partial_value, 'exp')  122 us
    all_to_all x1, waiting for transfers between devices, gather_outputs(): lax.all_to_all(out_part, 'seq', split_axis=0, concat_axis=0, tiled=True)  67 us
    all_to_all x2, local copies, waits for them, and re-layouts, to_owners(): lax.all_to_all(buffer, 'seq', split_axis=0, concat_axis=0, tiled=True)  17.1 us
    gather x2, local copies, waits for them, and re-layouts, shards(): sent_back = (d_out[owner_row] * filled[:, None]).reshape(n_seq, capacity, D)  15 us
    gather x2, local copies, waits for them, and re-layouts, shards(): normed[owner_row // TOPK] * filled[:, None]  14.9 us
    mul x3, local copies, waits for them, and re-layouts, shards(): route_gates[:, :, None] * residual_error[:, None, :]  11.7 us
  transfers between devices with their start and end apart: 4, of which 3 were waited for; matrix products, arithmetic and copies ran while one was open for 3% of the time, Pallas kernels for 0%

commit v1 on v0

--- a/solution.py
+++ b/solution.py
@@ -1,6 +1,10 @@
+import functools
+
 import jax
 import jax.numpy as jnp
 from jax import lax
+from jax.experimental import pallas as pl
+from jax.experimental.pallas import tpu as pltpu
 from jax.sharding import PartitionSpec as P
 
 D = 2880
@@ -13,6 +17,7 @@
 STEER = 6.5
 EPSILON = 1e-05
 MASKED = -1e30
+MESH = pl.DeviceIdType.MESH
 
 
 def passed_along(block, axis, distance):
@@ -71,6 +76,295 @@
         -1, width
     )
     return returned[flat_ids * capacity + slot_rank].astype(jnp.float32)
+
+
+def flipped(index, bit):
+    return index + bit - 2 * bit * ((index // bit) % 2)
+
+
+class Links:
+    def __init__(self, send_sem, recv_sem):
+        self.send_sem, self.recv_sem = send_sem, recv_sem
+        self.me = lax.axis_index("seq")
+        self.e = lax.axis_index("exp")
+        self.partner = flipped(self.me, 1)
+        self.across_x = flipped(self.me, 2)
+        self.across_y = flipped(self.me, 4)
+        self.diagonal = flipped(self.across_x, 4)
+        self.count = 0
+        self.started = []
+
+    def new(self, number=1):
+        first = self.count
+        self.count += number
+        return first
+
+    def copy(self, src, dst, index, seq=None, exp=None):
+        device = {"seq": self.me if seq is None else seq, "exp": self.e if exp is None else exp}
+        return pltpu.make_async_remote_copy(
+            src_ref=src,
+            dst_ref=dst,
+            send_sem=self.send_sem.at[index],
+            recv_sem=self.recv_sem.at[index],
+            device_id=device,
+            device_id_type=MESH,
+        )
+
+    def send(self, src, dst, index, **to):
+        sent = self.copy(src, dst, index, **to)
+        sent.start()
+        self.started.append(sent)
+
+    def arrived(self, dst, index):
+        self.copy(dst, dst, index, seq=self.partner).wait_recv()
+
+    def drain(self):
+        for sent in self.started:
+            sent.wait_send()
+
+
+def piece_of(e, k):
+    out = e
+    bit = 1
+    while bit <= k:
+        if k & bit:
+            out = flipped(out, bit)
+        bit *= 2
+    return out
+
+
+def greet(links, n_exp, all_seq, n_seq):
+    barrier = pltpu.get_barrier_semaphore()
+    peers = 0
+    flips = range(1, n_seq) if all_seq else [1, 2, 4]
+    for k in flips:
+        pl.semaphore_signal(
+            barrier, inc=1, device_id={"seq": piece_of(links.me, k), "exp": links.e}, device_id_type=MESH
+        )
+        peers += 1
+    for k in range(1, n_exp):
+        pl.semaphore_signal(
+            barrier, inc=1, device_id={"seq": links.me, "exp": piece_of(links.e, k)}, device_id_type=MESH
+        )
+        peers += 1
+    pl.semaphore_wait(barrier, peers)
+
+
+def spread(links, n_exp, own, everywhere, local_sem):
+    me, e = links.me, links.e
+    X, Y, C, D = links.across_x, links.across_y, links.partner, links.diagonal
+    z_id, x_id, y_id, c_id = (links.new(n_exp) for _ in range(4))
+    d_id, cx_id, cy_id, cd_id = (links.new(n_exp) for _ in range(4))
+    local = pltpu.make_async_copy(own, everywhere.at[me, e], local_sem)
+    local.start()
+
+    def launch(k):
+        spot = everywhere.at[me, piece_of(e, k)]
+        if k:
+            links.arrived(spot, z_id + k)
+        src = spot if k else own
+        links.send(src, spot, x_id + k, seq=X)
+        links.send(src, spot, y_id + k, seq=Y)
+        links.send(src, spot, c_id + k, seq=C)
+
+    def relay(k):
+        from_x = everywhere.at[X, piece_of(e, k)]
+        from_y = everywhere.at[Y, piece_of(e, k)]
+        links.arrived(from_x, x_id + k)
+        if k % 2 == 0:
+            links.send(from_x, from_x, d_id + k, seq=Y)
+        links.send(from_x, from_x, cx_id + k, seq=C)
+        links.arrived(from_y, y_id + k)
+        if k % 2:
+            links.send(from_y, from_y, d_id + k, seq=X)
+        links.send(from_y, from_y, cy_id + k, seq=C)
+
+    def last(k):
+        from_d = everywhere.at[D, piece_of(e, k)]
+        links.arrived(from_d, d_id + k)
+        links.send(from_d, from_d, cd_id + k, seq=C)
+
+    launch(0)
+    for k in range(1, n_exp):
+        links.send(own, everywhere.at[me, e], z_id + k, exp=piece_of(e, k))
+    for k in range(1, n_exp):
+        launch(k)
+        relay(k - 1)
+        if k > 1:
+            last(k - 2)
+    relay(n_exp - 1)
+    for k in range(max(n_exp - 2, 0), n_exp):
+        last(k)
+    for k in range(n_exp):
+        piece = piece_of(e, k)
+        links.arrived(everywhere.at[C, piece], c_id + k)
+        links.arrived(everywhere.at[flipped(C, 2), piece], cx_id + k)
+        links.arrived(everywhere.at[flipped(C, 4), piece], cy_id + k)
+        links.arrived(everywhere.at[flipped(flipped(C, 2), 4), piece], cd_id + k)
+    local.wait()
+
+
+def mix_kernel(
+    n_seq, n_exp, part, gates, gain, everywhere, mixed_out, gates_out, landed, own, send_sem, recv_sem, local_sem
+):
+    links = Links(send_sem, recv_sem)
+    me, e = links.me, links.e
+    greet(links, n_exp, True, n_seq)
+    r_id, g_id = links.new(n_exp), links.new(n_seq)
+    for k in range(1, n_exp):
+        links.send(part.at[piece_of(e, k)], landed.at[k - 1], r_id + k, exp=piece_of(e, k))
+    for k in range(1, n_seq):
+        peer = piece_of(me, k)
+        links.send(gates.at[peer], gates_out.at[me], g_id + k, seq=peer)
+    gates_out[me] = gates[me]
+    total = part[e].astype(jnp.float32)
+    for k in range(1, n_exp):
+        links.arrived(landed.at[k - 1], r_id + k)
+        total = total + landed[k - 1].astype(jnp.float32)
+    mixed_out[...] = total
+    scale = lax.rsqrt(jnp.mean(total * total, axis=-1, keepdims=True) + EPSILON)
+    own[...] = (total * scale * gain[...]).astype(jnp.bfloat16)
+    spread(links, n_exp, own, everywhere, local_sem)
+    for k in range(1, n_seq):
+        links.arrived(gates_out.at[piece_of(me, k)], g_id + k)
+    links.drain()
+
+
+def error_kernel(
+    n_exp, part, mixed, target, everywhere, pair, side, from_x, from_y, landed, own, send_sem, recv_sem, local_sem
+):
+    links = Links(send_sem, recv_sem)
+    me, e = links.me, links.e
+    core, chip = me % 2, me // 2
+    chip_x, chip_y = flipped(chip, 1), flipped(chip, 2)
+    chip_d = flipped(chip_x, 2)
+    X, Y, C = links.across_x, links.across_y, links.partner
+    greet(links, n_exp, False, 0)
+    p_id, d_id, x_id, y_id, z_id = (links.new(n_exp) for _ in range(5))
+    order = list(range(n_exp))[::-1]
+    for k in order:
+        links.send(part.at[:, 1 - core, piece_of(e, k)], pair.at[k], p_id + k, seq=C)
+    for k in order:
+        links.arrived(pair.at[k], p_id + k)
+        pair[k] = (pair[k].astype(jnp.float32) + part[:, core, piece_of(e, k)].astype(jnp.float32)).astype(
+            jnp.bfloat16
+        )
+        if k % 2 == 0:
+            links.send(pair.at[k, chip_d], side.at[k], d_id + k, seq=X)
+            links.send(pair.at[k, chip_x], from_x.at[k], x_id + k, seq=X)
+        else:
+            links.send(pair.at[k, chip_d], side.at[k], d_id + k, seq=Y)
+            links.send(pair.at[k, chip_y], from_y.at[k], y_id + k, seq=Y)
+    for k in order:
+        links.arrived(side.at[k], d_id + k)
+        onward = chip_y if k % 2 == 0 else chip_x
+        side[k] = (side[k].astype(jnp.float32) + pair[k, onward].astype(jnp.float32)).astype(jnp.bfloat16)
+        if k % 2 == 0:
+            links.send(side.at[k], from_y.at[k], y_id + k, seq=Y)
+        else:
+            links.send(side.at[k], from_x.at[k], x_id + k, seq=X)
+    total = None
+    for k in order:
+        links.arrived(from_x.at[k], x_id + k)
+        links.arrived(from_y.at[k], y_id + k)
+        total = (
+            pair[k, chip].astype(jnp.float32)
+            + from_x[k].astype(jnp.float32)
+            + from_y[k].astype(jnp.float32)
+        )
+        if k:
+            from_x[k] = total.astype(jnp.bfloat16)
+            links.send(from_x.at[k], landed.at[k - 1], z_id + k, exp=piece_of(e, k))
+    total = total + mixed[...] - target[...]
+    for k in order[:-1]:
+        links.arrived(landed.at[k - 1], z_id + k)
+        total = total + landed[k - 1].astype(jnp.float32)
+    own[...] = total.astype(jnp.bfloat16)
+    spread(links, n_exp, own, everywhere, local_sem)
+    links.drain()
+
+
+VM = pl.BlockSpec(memory_space=pltpu.VMEM)
+ANY = pl.BlockSpec(memory_space=pl.ANY)
+
+
+def dense(
+    heads_out, out_proj, residual, norm_gain, expert_ids, route_scores, w_gate_up, w_down, control
+):
+    n_seq, n_exp = lax.axis_size("seq"), lax.axis_size("exp")
+    seg_len, width = heads_out.shape[0], out_proj.shape[1]
+    sub = seg_len // n_exp
+    bf16, f32 = jnp.bfloat16, jnp.float32
+    partial_value = jnp.dot(heads_out, out_proj, preferred_element_type=f32)
+    column_width = residual.shape[1]
+    at = lax.axis_index("exp") * column_width
+    placed = lax.dynamic_update_slice_in_dim(jnp.zeros((seg_len, width), bf16), residual, at, 1)
+    part = (partial_value + placed.astype(f32)).astype(bf16).reshape(n_exp, sub, width)
+    route_gates = route_scores / jnp.sum(route_scores, axis=-1, keepdims=True)
+    member = expert_ids[None, :, :] == jnp.arange(n_seq, dtype=jnp.int32)[:, None, None]
+    gates = jnp.sum(jnp.where(member, route_gates[None], 0.0), axis=-1).reshape(n_seq, 1, seg_len)
+    spread_count = 8 * n_exp
+    rows, mixed, gates_mine = pl.pallas_call(
+        functools.partial(mix_kernel, n_seq, n_exp),
+        out_shape=(
+            jax.ShapeDtypeStruct((n_seq, n_exp, sub, width), bf16),
+            jax.ShapeDtypeStruct((sub, width), f32),
+            jax.ShapeDtypeStruct((n_seq, 1, seg_len), f32),
+        ),
+        in_specs=[VM, VM, VM],
+        out_specs=(ANY, VM, VM),
+        scratch_shapes=[
+            pltpu.VMEM((n_exp - 1, sub, width), bf16),
+            pltpu.VMEM((sub, width), bf16),
+            pltpu.SemaphoreType.DMA((spread_count + n_exp + n_seq,)),
+            pltpu.SemaphoreType.DMA((spread_count + n_exp + n_seq,)),
+            pltpu.SemaphoreType.DMA,
+        ],
+        compiler_params=pltpu.CompilerParams(collective_id=0, has_side_effects=True),
+        name="mix",
+    )(part, gates, norm_gain.reshape(1, width))
+    rows_flat = rows.reshape(n_seq * seg_len, width)
+    gate_col = gates_mine.reshape(n_seq * seg_len, 1)
+    down_slice = w_down[0]
+    gate_value = jnp.dot(rows_flat, w_gate_up[0, 0], preferred_element_type=f32)
+    up_value = jnp.dot(rows_flat, w_gate_up[0, 1], preferred_element_type=f32)
+    squashed = jax.nn.sigmoid(GLU_ALPHA * gate_value)
+    glu_value = gate_value * squashed
+    hidden = ((up_value + 1.0) * glu_value).astype(bf16)
+    out_part = (gate_col * jnp.dot(hidden, down_slice, preferred_element_type=f32)).astype(bf16)
+    target = (STEER * control / jnp.sqrt(jnp.sum(control * control))).reshape(1, width)
+    errors = pl.pallas_call(
+        functools.partial(error_kernel, n_exp),
+        out_shape=jax.ShapeDtypeStruct((n_seq, n_exp, sub, width), bf16),
+        in_specs=[VM, VM, VM],
+        out_specs=ANY,
+        scratch_shapes=[
+            pltpu.VMEM((n_exp, n_seq // 2, sub, width), bf16),
+            pltpu.VMEM((n_exp, sub, width), bf16),
+            pltpu.VMEM((n_exp, sub, width), bf16),
+            pltpu.VMEM((n_exp, sub, width), bf16),
+            pltpu.VMEM((n_exp - 1, sub, width), bf16),
+            pltpu.VMEM((sub, width), bf16),
+            pltpu.SemaphoreType.DMA((spread_count + 5 * n_exp,)),
+            pltpu.SemaphoreType.DMA((spread_count + 5 * n_exp,)),
+            pltpu.SemaphoreType.DMA,
+        ],
+        compiler_params=pltpu.CompilerParams(collective_id=1, has_side_effects=True),
+        name="error",
+    )(out_part.reshape(n_seq // 2, 2, n_exp, sub, width), mixed, target)
+    grads_in = errors.reshape(n_seq * seg_len, width)
+    d_hidden = gate_col * lax.dot_general(
+        grads_in, down_slice, (((1,), (1,)), ((), ())), preferred_element_type=f32
+    )
+    d_gate = (
+        d_hidden
+        * (up_value + 1.0)
+        * (squashed + GLU_ALPHA * gate_value * squashed * (1.0 - squashed))
+    ).astype(bf16)
+    d_up = (d_hidden * glu_value).astype(bf16)
+    grad_gate = lax.dot_general(rows_flat, d_gate, (((0,), (0,)), ((), ())), preferred_element_type=f32)
+    grad_up = lax.dot_general(rows_flat, d_up, (((0,), (0,)), ((), ())), preferred_element_type=f32)
+    return jnp.stack([grad_gate, grad_up])[None].astype(bf16)
 
 
 def shards(
@@ -93,6 +387,10 @@
     capacity = 2 * TOPK * seg_len // n_seq
     block_index = lax.axis_index("exp")
     heads_out = attend(queries, attn_keys, attn_values, sink_logits, doc_start)
+    if n_seq == 8 and capacity >= seg_len and lax.axis_size("exp") == 4:
+        return dense(
+            heads_out, out_proj, residual, norm_gain, expert_ids, route_scores, w_gate_up, w_down, control
+        )
     partial_value = jnp.dot(heads_out, out_proj, preferred_element_type=jnp.float32)
     column_width = residual.shape[1]
     own_columns = lax.dynamic_slice_in_dim(

time: 549 us -> 234 us (0.43); the launches traced: 539 us -> 233 us
  waiting for transfers between devices: 189 us -> 0.01 us
  Pallas kernels: 0 us -> 148 us
  blocking collectives: 142 us -> 0 us
  local copies, waits for them, and re-layouts: 99.9 us -> 18.1 us
  other arithmetic: 33.8 us -> 13.4 us
  between operations: 14.6 us -> 1.03 us
    pallas_call x0 -> x2, Pallas kernels: none -> 148 us  [the longest x1 82.7 us: dense(): pl.pallas_call(functools.partial(error_kernel, n_exp), out_shape=jax.Shap...]
    all_to_all x2 -> x0, blocking collectives: 142 us -> none  [to_owners(): lax.all_to_all(buffer, 'seq', split_axis=0, concat_axis=0, tiled=True)]
    psum x2 -> x0, waiting for transfers between devices: 122 us -> none  [slice_total(): return lax.psum(partial_value, 'exp')]
    all_to_all x1 -> x0, waiting for transfers between devices: 67 us -> none  [gather_outputs(): lax.all_to_all(out_part, 'seq', split_axis=0, concat_axis=0, tiled=True)]
    gather x5 -> x0, local copies, waits for them, and re-layouts: 39.2 us -> none  [the longest x2 15 us: shards(): sent_back = (d_out[owner_row] * filled[:, None]).reshape(n_seq, capacity, D)]
    all_to_all x3 -> x0, local copies, waits for them, and re-layouts: 25.4 us -> none  [the longest x2 17.1 us: to_owners(): lax.all_to_all(buffer, 'seq', split_axis=0, concat_axis=0, tiled=True)]
    mul x5 -> x0, local copies, waits for them, and re-layouts: 11.9 us -> none  [the longest x3 11.7 us: shards(): route_gates[:, :, None] * residual_error[:, None, :]]
    scatter x2 -> x0, local copies, waits for them, and re-layouts: 6.21 us -> none  [the longest x1 3.77 us: shards(): filled = jnp.zeros((n_seq * capacity,), jnp.bfloat16).at[slot_index].set(...]
  transfers between devices with their start and end apart: 4 -> 1, of which waited for: 3 -> 0; matrix products, arithmetic and copies ran while one was open for 3% -> 5% of each run, Pallas kernels for 0% -> 0%
where the time goes in v1:
time: 234 us; the launch traced here: 233 us
  Pallas kernels  148 us (63%)
  matrix products  50.1 us (21%)
  local copies, waits for them, and re-layouts  18.1 us (8%)
  other arithmetic  13.4 us (6%)
  starting transfers between devices  2.39 us (1%)
    pallas_call x1, Pallas kernels, dense(): pl.pallas_call(functools.partial(error_kernel, n_exp), out_shape=jax.Shap...  82.7 us
    pallas_call x1, Pallas kernels, dense(): pl.pallas_call(functools.partial(mix_kernel, n_seq, n_exp), out_shape=(ja...  65.6 us
    dot_general x1, matrix products, dense(): jnp.dot(hidden, down_slice, preferred_element_type=f32)  9.02 us
    dot_general x1, matrix products, dense(): lax.dot_general(rows_flat, d_gate, (((0,), (0,)), ((), ())), preferred_el...  8.65 us
    convert_element_type x1, local copies, waits for them, and re-layouts, dense(): (gate_col * jnp.dot(hidden, down_slice, preferred_element_type=f32)).asty...  8.47 us
    dot_general x1, matrix products, dense(): gate_value = jnp.dot(rows_flat, w_gate_up[0, 0], preferred_element_type=f32)  8.42 us
    dot_general x1, matrix products, dense(): lax.dot_general(grads_in, down_slice, (((1,), (1,)), ((), ())), preferred...  8.24 us
    another operation x1, other arithmetic, dense(): return jnp.stack([grad_gate, grad_up])[None].astype(bf16)  6.51 us
  transfers between devices with their start and end apart: 1, of which 0 were waited for; matrix products, arithmetic and copies ran while one was open for 5% of the time, Pallas kernels for 0%

profile of v1, /device:TPU:0, one launch (start us, length us, event | category | flops | bytes accessed | tf_op | source)
XLA Modules:
  0.0 233.3 jit_solution(16883854202929079232)
XLA Ops:
  0.0 0.8 pad_maximum_fusion.1
  0.8 2.4 %collective-permute-start = (bf16[2,128,128]{2,1,0:T(8,128)(2,1)S(1)}, bf16[2,128,128]{2,1,0:T(8,128)(2,1)S(1)}, u32[]{:S(2)}, u32[]{:S(2)}) collective-permute-start(bf16[2,128,128]{2,1,0:T(8,128)(2,1)S(1)} %pad_maximum_fusion.1), channel_id=1, source_target_pairs={{0,4},{4,8},{8,12},{12,16},{16,20},{20,24},{24,28},{1,5},{5,9},{9,... | collective-permute-start | bytes 196616 | tf_op jit(solution)/shard_map/ppermute | solution.py:26
  3.2 0.9 copy.37
  4.0 0.9 copy.35
  5.0 1.3 multiply_reduce_fusion
  7.0 0.7 max.18
  7.7 0.7 reduce_sum.37
  8.4 0.7 broadcast_divide_fusion
  9.1 1.3 reshape.190.gain
  10.4 0.7 multiply_divide_fusion
  11.1 0.6 reshape.193.target
  11.7 1.1 copy.38
  12.9 0.1 broadcast_in_dim.51
  13.0 1.0 constant_dynamic-update-slice_fusion
  13.9 0.8 compare_and_fusion
  14.7 1.3 select_reduce_fusion
  16.0 0.0 collective-permute-done
  16.0 0.1 copy.34
  16.1 0.1 copy.36
  16.2 0.5 fusion.13
  16.7 0.1 broadcast_maximum_fusion
  16.8 0.5 fusion.14
  17.3 0.1 exponential_add_fusion
  17.4 0.7 convolution_convert_fusion.2
  18.1 0.9 slice-done.5
  19.0 0.7 slice-done.6
  19.7 1.7 fusion.11
  21.4 1.2 copy.40
  22.6 65.6 %mix.1 = (bf16[8,4,32,2880]{3,2,1,0:T(8,128)(2,1)}, f32[32,2880]{1,0:T(8,128)}, f32[8,1,128]{2,1,0:T(1,128)}) custom-call(bf16[4,32,2880]{2,1,0:T(8,128)(2,1)} %bitcast.64, f32[8,1,128]{2,1,0:T(1,128)} %bitcast.72, f32[1,2880]{1,0:T(1,128)} %reshape.190.gain), custom_call_target="tpu_custom_call" | custom-call | tf_op jit(solution)/shard_map/mix/pallas_call | solution.py:307
  88.2 0.0 slice-start.1
  88.2 0.0 slice-start.2
  88.3 0.0 copy-start
  88.3 0.0 slice-start.7
  88.3 8.4 %fusion.5 = f32[1024,720]{0,1:T(8,128)S(1)} fusion(bf16[1024,2880]{1,0:T(8,128)(2,1)} %bitcast.75, bf16[1,2,2880,720]{2,3,1,0:T(8,128)(2,1)} %param.23), kind=kOutput, calls=%fused_computation.9 | convolution fusion | flops 4246732800 | bytes 13217792 | tf_op jit(solution)/shard_map/dot_general | solution.py:329
  96.7 0.0 slice-done
  96.8 0.0 slice-start.8
  96.8 6.4 %fusion.7 = f32[1024,720]{0,1:T(8,128)} fusion(bf16[1024,2880]{1,0:T(8,128)(2,1)S(1)} %bitcast.77, bf16[1,2,2880,720]{2,3,1,0:T(8,128)(2,1)S(1)} %bitcast.74), kind=kOutput, calls=%fused_computation.11 | convolution fusion | flops 4246732800 | bytes 13217792 | tf_op jit(solution)/shard_map/dot_general | solution.py:330
  103.2 0.0 slice-done.7
  103.2 0.0 copy-done.1
  103.2 9.0 %multiply_convert_fusion = bf16[1024,2880]{0,1:T(8,128)(2,1)} fusion(f32[1024]{0:T(1024)S(1)} %bitcast.85, bf16[1,720,2880]{2,1,0:T(8,128)(2,1)S(1)} %bitcast.84, f32[1024,720]{0,1:T(8,128)} %fusion.7, f32[1024,720]{0,1:T(8,128)S(1)} %fusion.5), kind=kOutput, calls=%fused_computation | convolution fusion | flops 4258529280 | bytes 15947776 | tf_op jit(solution)/shard_map/dot_general | solution.py:334
  112.2 8.5 %copy.41 = bf16[1024,2880]{1,0:T(8,128)(2,1)} copy(bf16[1024,2880]{0,1:T(8,128)(2,1)} %multiply_convert_fusion) | data formatting | bytes 11796480 | tf_op jit(solution)/shard_map/convert_element_type | solution.py:334
  120.7 82.7 %error.1 = bf16[8,4,32,2880]{3,2,1,0:T(8,128)(2,1)} custom-call(bf16[4,2,4,32,2880]{4,3,2,1,0:T(8,128)(2,1)} %bitcast.62, f32[32,2880]{1,0:T(8,128)} %get-tuple-element.10.mixed, f32[1,2880]{1,0:T(1,128)} %reshape.193.target), custom_call_target="tpu_custom_call" | custom-call | tf_op jit(solution)/shard_map/error/pallas_call | solution.py:336
  203.4 0.0 slice-start.3
  203.4 8.2 %fusion.2 = f32[1024,720]{0,1:T(8,128)S(1)} fusion(bf16[1024,2880]{1,0:T(8,128)(2,1)} %bitcast.63, bf16[1,720,2880]{2,1,0:T(8,128)(2,1)} %param.24), kind=kOutput, calls=%fused_computation.6 | convolution fusion | flops 4246732800 | bytes 12994560 | tf_op jit(solution)/shard_map/dot_general | solution.py:356
  211.7 0.0 slice-start.4
  211.7 8.7 %fusion = bf16[1,1,2880,720]{2,3,1,0:T(8,128)(2,1)S(1)} fusion(bf16[1024,2880]{1,0:T(8,128)(2,1)} %bitcast.76, f32[1024,720]{0,1:T(8,128)S(1)} %fusion.2, f32[1024,720]{0,1:T(8,128)S(1)} %copy-done.3, f32[1024,720]{0,1:T(8,128)S(1)} %copy-done.4, f32[1024]{0:T(1024)S(1)} %bitcast.86), kind=kOutput, calls=%fused_computation.4 | convolution fusion | flops 4258391040 | bytes 18896896 | tf_op jit(solution)/shard_map/dot_general | solution.py:365
  220.4 6.4 %fusion.1 = bf16[1,1,2880,720]{2,3,1,0:T(8,128)(2,1)} fusion(bf16[1024,2880]{1,0:T(8,128)(2,1)S(1)} %bitcast.80, f32[1024,720]{0,1:T(8,128)S(1)} %fusion.2, f32[1024]{0:T(1024)S(1)} %bitcast.87, f32[1024,720]{0,1:T(8,128)S(1)} %copy-done.3), kind=kOutput, calls=%fused_computation.5 | convolution fusion | flops 4254704640 | bytes 15947776 | tf_op jit(solution)/shard_map/dot_general | solution.py:366
  226.8 6.5 %pad_maximum_fusion = bf16[1,2,2880,720]{2,3,1,0:T(8,128)(2,1)} fusion(bf16[1,1,2880,720]{2,3,1,0:T(8,128)(2,1)} %fusion.1, bf16[1,1,2880,720]{2,3,1,0:T(8,128)(2,1)S(1)} %fusion), kind=kLoop, calls=%fused_computation.1 | loop fusion | flops 4147200 | bytes 16588800 | tf_op jit(solution)/shard_map/stack | solution.py:367
  (23 shorter events, 0.0 us)
Async XLA Ops:
  0.8 15.2 %collective-permute-start = (bf16[2,128,128]{2,1,0:T(8,128)(2,1)S(1)}, bf16[2,128,128]{2,1,0:T(8,128)(2,1)S(1)}, u32[]{:S(2)}, u32[]{:S(2)}) collective-permute-start(bf16[2,128,128]{2,1,0:T(8,128)(2,1)S(1)} %pad_maximum_fusion.1), channel_id=1, source_target_pairs={{0,4},{4,8},{8,12},{12,16},{16,20},{20,24},{24,28},{1,5},{5,9},{9,... | collective-permute-start | bytes 196616 | tf_op jit(solution)/shard_map/ppermute | solution.py:26
  16.8 2.2 slice-start.5
  17.4 2.3 slice-start.6
  22.6 74.1 %slice-start = ((s8[8478720]{0:T(1024)(128)(4,1)}), s8[90112]{0:T(1024)(128)(4,1)S(1)}, s32[]{:S(2)}) async-start(s8[8478720]{0:T(1024)(128)(4,1)} %bitcast.73), calls=%async_computation | async-start | bytes 180224
  88.2 8.5 %slice-start.1 = ((s8[8478720]{0:T(1024)(128)(4,1)}), s8[4194304]{0:T(1024)(128)(4,1)S(1)}, s32[]{:S(2)}) async-start(s8[8478720]{0:T(1024)(128)(4,1)} %bitcast.73), calls=%async_computation.1 | async-start | bytes 8388608
  88.2 8.5 %slice-start.2 = ((s8[8478720]{0:T(1024)(128)(4,1)}), s8[4194304]{0:T(1024)(128)(4,1)S(1)}, s32[]{:S(2)}) async-start(s8[8478720]{0:T(1024)(128)(4,1)} %bitcast.73), calls=%async_computation.2 | async-start | bytes 8388608
  88.3 8.5 %copy-start = (bf16[8,4,32,2880]{3,2,1,0:T(8,128)(2,1)S(1)}, bf16[8,4,32,2880]{3,2,1,0:T(8,128)(2,1)}, u32[]{:S(2)}) copy-start(bf16[8,4,32,2880]{3,2,1,0:T(8,128)(2,1)} %get-tuple-element.8) | copy-start | bytes 17694724
  88.3 14.9 %slice-start.7 = ((s8[4239360]{0:T(1024)(128)(4,1)}), s8[4194304]{0:T(1024)(128)(4,1)S(1)}, s32[]{:S(2)}) async-start(s8[4239360]{0:T(1024)(128)(4,1)} %bitcast.83), calls=%async_computation.7 | async-start | bytes 8388608
  96.8 6.4 %copy-start.2 = (f32[1024,720]{0,1:T(8,128)}, f32[1024,720]{0,1:T(8,128)S(1)}, u32[]{:S(2)}) copy-start(f32[1024,720]{0,1:T(8,128)S(1)} %fusion.5) | copy-start | bytes 8847364
  96.8 6.4 %slice-start.8 = ((s8[4239360]{0:T(1024)(128)(4,1)}), s8[45056]{0:T(1024)(128)(4,1)S(1)}, s32[]{:S(2)}) async-start(s8[4239360]{0:T(1024)(128)(4,1)} %bitcast.83), calls=%async_computation.8 | async-start | bytes 90112
  96.8 6.4 %copy-start.1 = (f32[8,1,128]{2,1,0:T(1,128)S(1)}, f32[8,1,128]{2,1,0:T(1,128)}, u32[]{:S(2)}) copy-start(f32[8,1,128]{2,1,0:T(1,128)} %get-tuple-element.9) | copy-start | bytes 12292
  203.4 8.3 %copy-start.3 = (f32[1024,720]{0,1:T(8,128)S(1)}, f32[1024,720]{0,1:T(8,128)}, u32[]{:S(2)}) copy-start(f32[1024,720]{0,1:T(8,128)} %copy-done.2) | copy-start | bytes 8847364
  203.4 8.3 %copy-start.4 = (f32[1024,720]{0,1:T(8,128)S(1)}, f32[1024,720]{0,1:T(8,128)}, u32[]{:S(2)}) copy-start(f32[1024,720]{0,1:T(8,128)} %fusion.7) | copy-start | bytes 8847364
  203.4 17.0 %slice-start.3 = ((s8[6029312]{0:T(1024)(128)(4,1)}), s8[4194304]{0:T(1024)(128)(4,1)S(1)}, s32[]{:S(2)}) async-start(s8[6029312]{0:T(1024)(128)(4,1)} %bitcast.78), calls=%async_computation.3 | async-start | bytes 8388608
  211.7 8.7 %slice-start.4 = ((s8[6029312]{0:T(1024)(128)(4,1)}), s8[1835008]{0:T(1024)(128)(4,1)S(1)}, s32[]{:S(2)}) async-start(s8[6029312]{0:T(1024)(128)(4,1)} %bitcast.78), calls=%async_computation.4 | async-start | bytes 3670016

commit v2 on v1

--- a/solution.py
+++ b/solution.py
@@ -150,16 +150,16 @@
     pl.semaphore_wait(barrier, peers)
 
 
-def spread(links, n_exp, own, everywhere, local_sem):
+def spread(links, n_exp, own, everywhere, local_sem, consume):
     me, e = links.me, links.e
     X, Y, C, D = links.across_x, links.across_y, links.partner, links.diagonal
     z_id, x_id, y_id, c_id = (links.new(n_exp) for _ in range(4))
     d_id, cx_id, cy_id, cd_id = (links.new(n_exp) for _ in range(4))
-    local = pltpu.make_async_copy(own, everywhere.at[me, e], local_sem)
+    local = pltpu.make_async_copy(own, everywhere.at[e, me], local_sem)
     local.start()
 
     def launch(k):
-        spot = everywhere.at[me, piece_of(e, k)]
+        spot = everywhere.at[piece_of(e, k), me]
         if k:
             links.arrived(spot, z_id + k)
         src = spot if k else own
@@ -168,8 +168,8 @@
         links.send(src, spot, c_id + k, seq=C)
 
     def relay(k):
-        from_x = everywhere.at[X, piece_of(e, k)]
-        from_y = everywhere.at[Y, piece_of(e, k)]
+        from_x = everywhere.at[piece_of(e, k), X]
+        from_y = everywhere.at[piece_of(e, k), Y]
         links.arrived(from_x, x_id + k)
         if k % 2 == 0:
             links.send(from_x, from_x, d_id + k, seq=Y)
@@ -180,35 +180,70 @@
         links.send(from_y, from_y, cy_id + k, seq=C)
 
     def last(k):
-        from_d = everywhere.at[D, piece_of(e, k)]
+        from_d = everywhere.at[piece_of(e, k), D]
         links.arrived(from_d, d_id + k)
         links.send(from_d, from_d, cd_id + k, seq=C)
 
+    def finish(k):
+        piece = everywhere.at[piece_of(e, k)]
+        links.arrived(piece.at[C], c_id + k)
+        links.arrived(piece.at[flipped(C, 2)], cx_id + k)
+        links.arrived(piece.at[flipped(C, 4)], cy_id + k)
+        links.arrived(piece.at[flipped(flipped(C, 2), 4)], cd_id + k)
+        if k == 0:
+            local.wait()
+        consume(k)
+
     launch(0)
     for k in range(1, n_exp):
-        links.send(own, everywhere.at[me, e], z_id + k, exp=piece_of(e, k))
+        links.send(own, everywhere.at[e, me], z_id + k, exp=piece_of(e, k))
     for k in range(1, n_exp):
         launch(k)
         relay(k - 1)
         if k > 1:
             last(k - 2)
     relay(n_exp - 1)
-    for k in range(max(n_exp - 2, 0), n_exp):
-        last(k)
-    for k in range(n_exp):
-        piece = piece_of(e, k)
-        links.arrived(everywhere.at[C, piece], c_id + k)
-        links.arrived(everywhere.at[flipped(C, 2), piece], cx_id + k)
-        links.arrived(everywhere.at[flipped(C, 4), piece], cy_id + k)
-        links.arrived(everywhere.at[flipped(flipped(C, 2), 4), piece], cd_id + k)
-    local.wait()
+    last(n_exp - 2)
+    finish(0)
+    last(n_exp - 1)
+    for k in range(1, n_exp):
+        finish(k)
+
+
+def tile_of(size, most=256):
+    return next(t for t in range(most, 0, -1) if size % t == 0 and t % 16 == 0)
+
+
+def times_rows(weights, rows):
+    return lax.dot_general(weights, rows, (((1,), (1,)), ((), ())), preferred_element_type=jnp.float32)
 
 
 def mix_kernel(
-    n_seq, n_exp, part, gates, gain, everywhere, mixed_out, gates_out, landed, own, send_sem, recv_sem, local_sem
+    n_seq,
+    n_exp,
+    part,
+    gates,
+    gain,
+    weights_in,
+    rows_out,
+    mixed_out,
+    gates_out,
+    hidden_out,
+    by_gate_out,
+    by_up_out,
+    weights,
+    everywhere,
+    landed,
+    own,
+    send_sem,
+    recv_sem,
+    local_sem,
+    rows_sem,
 ):
     links = Links(send_sem, recv_sem)
     me, e = links.me, links.e
+    load = pltpu.make_async_copy(weights_in, weights, local_sem.at[1])
+    load.start()
     greet(links, n_exp, True, n_seq)
     r_id, g_id = links.new(n_exp), links.new(n_seq)
     for k in range(1, n_exp):
@@ -224,14 +259,66 @@
     mixed_out[...] = total
     scale = lax.rsqrt(jnp.mean(total * total, axis=-1, keepdims=True) + EPSILON)
     own[...] = (total * scale * gain[...]).astype(jnp.bfloat16)
-    spread(links, n_exp, own, everywhere, local_sem)
+    ff, width = weights.shape[1:]
+    tile = tile_of(ff)
+    stores = []
+
+    def consume(k):
+        piece = piece_of(e, k)
+        if k == 0:
+            load.wait()
+        store = pltpu.make_async_copy(everywhere.at[piece], rows_out.at[piece], rows_sem.at[k])
+        store.start()
+        stores.append(store)
+
+        def step(index, carry):
+            at = pl.ds(pl.multiple_of(index * tile, 16), tile)
+            rows = everywhere[piece].reshape(-1, width)
+            gate_value = times_rows(weights[0, at, :], rows)
+            up_value = times_rows(weights[1, at, :], rows)
+            squashed = jax.nn.sigmoid(GLU_ALPHA * gate_value)
+            glu_value = gate_value * squashed
+            hidden_out[piece, at, :] = ((up_value + 1.0) * glu_value).astype(jnp.bfloat16)
+            by_gate_out[piece, at, :] = (up_value + 1.0) * (
+                squashed + GLU_ALPHA * gate_value * squashed * (1.0 - squashed)
+            )
+            by_up_out[piece, at, :] = glu_value
+            return carry
+
+        lax.fori_loop(0, ff // tile, step, 0)
+
+    spread(links, n_exp, own, everywhere, local_sem.at[0], consume)
     for k in range(1, n_seq):
         links.arrived(gates_out.at[piece_of(me, k)], g_id + k)
     links.drain()
+    for store in stores:
+        store.wait()
 
 
 def error_kernel(
-    n_exp, part, mixed, target, everywhere, pair, side, from_x, from_y, landed, own, send_sem, recv_sem, local_sem
+    n_seq,
+    n_exp,
+    hidden,
+    gate_col,
+    gate_row,
+    weights,
+    by_gate_in,
+    by_up_in,
+    mixed,
+    target,
+    grads_out,
+    factors,
+    everywhere,
+    part,
+    pair,
+    side,
+    from_x,
+    from_y,
+    landed,
+    own,
+    send_sem,
+    recv_sem,
+    local_sem,
 ):
     links = Links(send_sem, recv_sem)
     me, e = links.me, links.e
@@ -239,23 +326,41 @@
     chip_x, chip_y = flipped(chip, 1), flipped(chip, 2)
     chip_d = flipped(chip_x, 2)
     X, Y, C = links.across_x, links.across_y, links.partner
+    ff, width = weights.shape
+    sub = mixed.shape[0]
+    tile = tile_of(ff)
+    loads = [
+        pltpu.make_async_copy(ref, factors.at[number], local_sem.at[1 + number])
+        for number, ref in enumerate((by_gate_in, by_up_in))
+    ]
+    for load in loads:
+        load.start()
     greet(links, n_exp, False, 0)
     p_id, d_id, x_id, y_id, z_id = (links.new(n_exp) for _ in range(5))
     order = list(range(n_exp))[::-1]
-    for k in order:
-        links.send(part.at[:, 1 - core, piece_of(e, k)], pair.at[k], p_id + k, seq=C)
-    for k in order:
+
+    def produce(k):
+        piece = piece_of(e, k)
+        for start in range(0, width, 512):
+            columns = slice(start, min(width, start + 512))
+            outs = lax.dot_general(
+                hidden[piece], weights[:, columns], (((0,), (0,)), ((), ())), preferred_element_type=jnp.float32
+            )
+            outs = (outs * gate_col[piece]).astype(jnp.bfloat16)
+            part[k, :, :, :, columns] = outs.reshape(n_seq // 2, 2, sub, -1)
+        links.send(part.at[k, :, 1 - core], pair.at[k], p_id + k, seq=C)
+
+    def merge(k):
         links.arrived(pair.at[k], p_id + k)
-        pair[k] = (pair[k].astype(jnp.float32) + part[:, core, piece_of(e, k)].astype(jnp.float32)).astype(
-            jnp.bfloat16
-        )
+        pair[k] = (pair[k].astype(jnp.float32) + part[k, :, core].astype(jnp.float32)).astype(jnp.bfloat16)
         if k % 2 == 0:
             links.send(pair.at[k, chip_d], side.at[k], d_id + k, seq=X)
             links.send(pair.at[k, chip_x], from_x.at[k], x_id + k, seq=X)
         else:
             links.send(pair.at[k, chip_d], side.at[k], d_id + k, seq=Y)
             links.send(pair.at[k, chip_y], from_y.at[k], y_id + k, seq=Y)
-    for k in order:
+
+    def pass_on(k):
         links.arrived(side.at[k], d_id + k)
         onward = chip_y if k % 2 == 0 else chip_x
         side[k] = (side[k].astype(jnp.float32) + pair[k, onward].astype(jnp.float32)).astype(jnp.bfloat16)
@@ -263,8 +368,8 @@
             links.send(side.at[k], from_y.at[k], y_id + k, seq=Y)
         else:
             links.send(side.at[k], from_x.at[k], x_id + k, seq=X)
-    total = None
-    for k in order:
+
+    def collect(k):
         links.arrived(from_x.at[k], x_id + k)
         links.arrived(from_y.at[k], y_id + k)
         total = (
@@ -275,12 +380,39 @@
         if k:
             from_x[k] = total.astype(jnp.bfloat16)
             links.send(from_x.at[k], landed.at[k - 1], z_id + k, exp=piece_of(e, k))
-    total = total + mixed[...] - target[...]
+        return total
+
+    produce(order[0])
+    for before, k in zip(order, order[1:]):
+        produce(k)
+        merge(before)
+    merge(order[-1])
+    pass_on(order[0])
+    for before, k in zip(order, order[1:]):
+        pass_on(k)
+        collect(before)
+    total = collect(0) + mixed[...] - target[...]
     for k in order[:-1]:
         links.arrived(landed.at[k - 1], z_id + k)
         total = total + landed[k - 1].astype(jnp.float32)
     own[...] = total.astype(jnp.bfloat16)
-    spread(links, n_exp, own, everywhere, local_sem)
+    for load in loads:
+        load.wait()
+
+    def consume(k):
+        piece = piece_of(e, k)
+        lanes = pl.ds(pl.multiple_of(piece * (n_seq * sub), n_seq * sub), n_seq * sub)
+
+        def step(index, carry):
+            at = pl.ds(pl.multiple_of(index * tile, 16), tile)
+            d_hidden = times_rows(weights[at, :], everywhere[piece].reshape(-1, width)) * gate_row[piece]
+            grads_out[0, at, lanes] = (d_hidden * factors[0, piece, at, :]).astype(jnp.bfloat16)
+            grads_out[1, at, lanes] = (d_hidden * factors[1, piece, at, :]).astype(jnp.bfloat16)
+            return carry
+
+        lax.fori_loop(0, ff // tile, step, 0)
+
+    spread(links, n_exp, own, everywhere, local_sem.at[0], consume)
     links.drain()
 
 
@@ -304,41 +436,44 @@
     member = expert_ids[None, :, :] == jnp.arange(n_seq, dtype=jnp.int32)[:, None, None]
     gates = jnp.sum(jnp.where(member, route_gates[None], 0.0), axis=-1).reshape(n_seq, 1, seg_len)
     spread_count = 8 * n_exp
-    rows, mixed, gates_mine = pl.pallas_call(
+    ff = w_down.shape[1]
+    group = n_seq * sub
+    rows, mixed, gates_mine, hidden, by_gate, by_up = pl.pallas_call(
         functools.partial(mix_kernel, n_seq, n_exp),
         out_shape=(
-            jax.ShapeDtypeStruct((n_seq, n_exp, sub, width), bf16),
+            jax.ShapeDtypeStruct((n_exp, n_seq, sub, width), bf16),
             jax.ShapeDtypeStruct((sub, width), f32),
             jax.ShapeDtypeStruct((n_seq, 1, seg_len), f32),
+            jax.ShapeDtypeStruct((n_exp, ff, group), bf16),
+            jax.ShapeDtypeStruct((n_exp, ff, group), f32),
+            jax.ShapeDtypeStruct((n_exp, ff, group), f32),
         ),
-        in_specs=[VM, VM, VM],
-        out_specs=(ANY, VM, VM),
+        in_specs=[VM, VM, VM, ANY],
+        out_specs=(ANY, VM, VM, VM, VM, VM),
         scratch_shapes=[
+            pltpu.VMEM((2, ff, width), bf16),
+            pltpu.VMEM((n_exp, n_seq, sub, width), bf16),
             pltpu.VMEM((n_exp - 1, sub, width), bf16),
             pltpu.VMEM((sub, width), bf16),
             pltpu.SemaphoreType.DMA((spread_count + n_exp + n_seq,)),
             pltpu.SemaphoreType.DMA((spread_count + n_exp + n_seq,)),
-            pltpu.SemaphoreType.DMA,
+            pltpu.SemaphoreType.DMA((2,)),
+            pltpu.SemaphoreType.DMA((n_exp,)),
         ],
         compiler_params=pltpu.CompilerParams(collective_id=0, has_side_effects=True),
         name="mix",
-    )(part, gates, norm_gain.reshape(1, width))
-    rows_flat = rows.reshape(n_seq * seg_len, width)
-    gate_col = gates_mine.reshape(n_seq * seg_len, 1)
-    down_slice = w_down[0]
-    gate_value = jnp.dot(rows_flat, w_gate_up[0, 0], preferred_element_type=f32)
-    up_value = jnp.dot(rows_flat, w_gate_up[0, 1], preferred_element_type=f32)
-    squashed = jax.nn.sigmoid(GLU_ALPHA * gate_value)
-    glu_value = gate_value * squashed
-    hidden = ((up_value + 1.0) * glu_value).astype(bf16)
-    out_part = (gate_col * jnp.dot(hidden, down_slice, preferred_element_type=f32)).astype(bf16)
+    )(part, gates, norm_gain.reshape(1, width), jnp.swapaxes(w_gate_up[0], 1, 2))
+    gate_flat = gates_mine.reshape(n_seq, n_exp, sub).transpose(1, 0, 2).reshape(n_exp, group)
     target = (STEER * control / jnp.sqrt(jnp.sum(control * control))).reshape(1, width)
-    errors = pl.pallas_call(
-        functools.partial(error_kernel, n_exp),
-        out_shape=jax.ShapeDtypeStruct((n_seq, n_exp, sub, width), bf16),
-        in_specs=[VM, VM, VM],
-        out_specs=ANY,
+    d_both = pl.pallas_call(
+        functools.partial(error_kernel, n_seq, n_exp),
+        out_shape=jax.ShapeDtypeStruct((2, ff, n_exp * group), bf16),
+        in_specs=[VM, VM, VM, VM, ANY, ANY, VM, VM],
+        out_specs=VM,
         scratch_shapes=[
+            pltpu.VMEM((2, n_exp, ff, group), f32),
+            pltpu.VMEM((n_exp, n_seq, sub, width), bf16),
+            pltpu.VMEM((n_exp, n_seq // 2, 2, sub, width), bf16),
             pltpu.VMEM((n_exp, n_seq // 2, sub, width), bf16),
             pltpu.VMEM((n_exp, sub, width), bf16),
             pltpu.VMEM((n_exp, sub, width), bf16),
@@ -347,24 +482,18 @@
             pltpu.VMEM((sub, width), bf16),
             pltpu.SemaphoreType.DMA((spread_count + 5 * n_exp,)),
             pltpu.SemaphoreType.DMA((spread_count + 5 * n_exp,)),
-            pltpu.SemaphoreType.DMA,
+            pltpu.SemaphoreType.DMA((3,)),
         ],
         compiler_params=pltpu.CompilerParams(collective_id=1, has_side_effects=True),
         name="error",
-    )(out_part.reshape(n_seq // 2, 2, n_exp, sub, width), mixed, target)
-    grads_in = errors.reshape(n_seq * seg_len, width)
-    d_hidden = gate_col * lax.dot_general(
-        grads_in, down_slice, (((1,), (1,)), ((), ())), preferred_element_type=f32
-    )
-    d_gate = (
-        d_hidden
-        * (up_value + 1.0)
-        * (squashed + GLU_ALPHA * gate_value * squashed * (1.0 - squashed))
-    ).astype(bf16)
-    d_up = (d_hidden * glu_value).astype(bf16)
-    grad_gate = lax.dot_general(rows_flat, d_gate, (((0,), (0,)), ((), ())), preferred_element_type=f32)
-    grad_up = lax.dot_general(rows_flat, d_up, (((0,), (0,)), ((), ())), preferred_element_type=f32)
-    return jnp.stack([grad_gate, grad_up])[None].astype(bf16)
+    )(hidden, gate_flat[:, :, None], gate_flat[:, None, :], w_down[0], by_gate, by_up, mixed, target)
+    grads = lax.dot_general(
+        d_both.reshape(2 * ff, n_exp * group),
+        rows.reshape(n_exp * group, width),
+        (((1,), (0,)), ((), ())),
+        preferred_element_type=f32,
+    )
+    return jnp.swapaxes(grads.astype(bf16).reshape(2, ff, width), 1, 2)[None]
 
 
 def shards(

time: 234 us -> 209 us (0.89)
  matrix products: 50.1 us -> 17.6 us
  Pallas kernels: 148 us -> 167 us
  local copies, waits for them, and re-layouts: 18.1 us -> 12.1 us
  other arithmetic: 13.4 us -> 8.24 us
    dot_general x6 -> x1, matrix products: 47.1 us -> 14.7 us  [dense(): lax.dot_general(d_both.reshape(2 * ff, n_exp * group), rows.reshape(n_exp...]
    pallas_call x1, Pallas kernels: 65.6 us -> 75.1 us  [dense(): pl.pallas_call(functools.partial(mix_kernel, n_seq, n_exp), out_shape=(ja...]
    pallas_call x1, Pallas kernels: 82.7 us -> 92.1 us  [dense(): pl.pallas_call(functools.partial(error_kernel, n_seq, n_exp), out_shape=j...]
    convert_element_type x1 -> x0, local copies, waits for them, and re-layouts: 8.47 us -> none  [dense(): (gate_col * jnp.dot(hidden, down_slice, preferred_element_type=f32)).asty...]
    another operation x1 -> x0, other arithmetic: 6.51 us -> none  [dense(): return jnp.stack([grad_gate, grad_up])[None].astype(bf16)]
  transfers between devices with their start and end apart: 1 -> 1, of which waited for: 0 -> 0; matrix products, arithmetic and copies ran while one was open for 5% -> 6% of each run, Pallas kernels for 0% -> 0%
where the time goes in v2:
time: 209 us; the launch traced here: 208 us
  Pallas kernels  167 us (80%)
  matrix products  17.6 us (8%)
  local copies, waits for them, and re-layouts  12.1 us (6%)
  other arithmetic  8.24 us (4%)
  starting transfers between devices  2.39 us (1%)
    pallas_call x1, Pallas kernels, dense(): pl.pallas_call(functools.partial(error_kernel, n_seq, n_exp), out_shape=j...  92.1 us
    pallas_call x1, Pallas kernels, dense(): pl.pallas_call(functools.partial(mix_kernel, n_seq, n_exp), out_shape=(ja...  75.1 us
    dot_general x1, matrix products, dense(): lax.dot_general(d_both.reshape(2 * ff, n_exp * group), rows.reshape(n_exp...  14.7 us
    unnamed x7, local copies, waits for them, and re-layouts  4.43 us
  transfers between devices with their start and end apart: 1, of which 0 were waited for; matrix products, arithmetic and copies ran while one was open for 6% of the time, Pallas kernels for 0%

profile of v2, /device:TPU:0, one launch (start us, length us, event | category | flops | bytes accessed | tf_op | source)
XLA Modules:
  0.0 208.4 jit_solution(5432852346023330197)
XLA Ops:
  0.0 0.8 pad_maximum_fusion
  0.8 2.4 %collective-permute-start = (bf16[2,128,128]{2,1,0:T(8,128)(2,1)S(1)}, bf16[2,128,128]{2,1,0:T(8,128)(2,1)S(1)}, u32[]{:S(2)}, u32[]{:S(2)}) collective-permute-start(bf16[2,128,128]{2,1,0:T(8,128)(2,1)S(1)} %pad_maximum_fusion), channel_id=1, source_target_pairs={{0,4},{4,8},{8,12},{12,16},{16,20},{20,24},{24,28},{1,5},{5,9},{9,... | collective-permute-start | bytes 196616 | tf_op jit(solution)/shard_map/ppermute | solution.py:26
  3.2 0.9 copy.38
  4.0 0.9 copy.36
  5.0 1.3 multiply_reduce_fusion
  7.0 0.7 max.18
  7.7 0.7 reduce_sum.37
  8.4 0.7 broadcast_divide_fusion
  9.1 1.3 reshape.157.gain
  10.4 0.7 multiply_divide_fusion
  11.1 0.6 reshape.159.target
  11.7 1.1 copy.39
  12.9 0.1 broadcast_in_dim.53
  13.0 1.0 constant_dynamic-update-slice_fusion
  13.9 0.8 compare_and_fusion
  14.7 1.3 select_reduce_fusion
  16.0 0.0 collective-permute-done
  16.0 0.1 copy.35
  16.1 0.1 copy.37
  16.2 0.5 fusion.1
  16.7 0.1 broadcast_maximum_fusion
  16.8 0.0 slice-start
  16.8 0.5 fusion.2
  17.3 0.1 exponential_add_fusion
  17.4 0.0 slice-start.1
  17.4 0.7 convolution_convert_fusion.1
  18.1 0.9 slice-done
  19.0 0.7 slice-done.1
  19.7 1.7 fusion
  21.4 1.2 copy.41
  22.6 75.1 %mix.1 = (bf16[4,8,32,2880]{3,2,1,0:T(8,128)(2,1)}, f32[32,2880]{1,0:T(8,128)}, f32[8,1,128]{2,1,0:T(1,128)}, bf16[4,720,256]{2,1,0:T(8,128)(2,1)}, f32[4,720,256]{2,1,0:T(8,128)}, /*index=5*/f32[4,720,256]{2,1,0:T(8,128)}) custom-call(bf16[4,32,2880]{2,1,0:T(8,128)(2,1)} %bitcast.56, f32[8,1,128]{2,1,0:T(1,128)} %bitcast.67, f32[1,2880]{1,0:T(1,128)} %reshape.157.gain, ...), custom_call_target="tpu_custom_call" | custom-call | tf_op jit(solution)/shard_map/mix/pallas_call | solution.py:441
  97.7 0.5 broadcast.97
  98.2 1.3 reduce.3
  99.5 0.1 reshape.158
  99.6 0.7 broadcast_in_dim_reshape.7.gate_row
  100.3 1.3 broadcast_in_dim_reshape.8.gate_col
  101.6 92.1 %error.1 = bf16[2,720,1024]{2,1,0:T(8,128)(2,1)} custom-call(bf16[4,720,256]{2,1,0:T(8,128)(2,1)} %get-tuple-element.11.hidden, f32[4,256,1]{2,1,0:T(8,128)} %broadcast_in_dim_reshape.8.gate_col, f32[4,1,256]{2,1,0:T(1,128)} %broadcast_in_dim_reshape.7.gate_row, bf16[720,2880]{1,0:T(8,128)(2,1)} %bitcast.55, f32[4,720,256]{2,1,0:T(8,128)} %get-tuple-element.13.by_gate_in, ...), custom_call_target="tpu_custom_call" | custom-call | tf_op jit(solution)/shard_map/error/pallas_call | solution.py:468
  193.7 14.7 %convolution_convert_fusion = bf16[1440,2880]{1,0:T(8,128)(2,1)} fusion(bf16[1440,1024]{1,0:T(8,128)(2,1)} %bitcast.57, bf16[1024,2880]{1,0:T(8,128)(2,1)} %bitcast.68), kind=kOutput, calls=%fused_computation | convolution fusion | flops 8497612800 | bytes 17141760 | tf_op jit(solution)/shard_map/dot_general | solution.py:490
  (5 shorter events, 0.0 us)
Async XLA Ops:
  0.8 15.2 %collective-permute-start = (bf16[2,128,128]{2,1,0:T(8,128)(2,1)S(1)}, bf16[2,128,128]{2,1,0:T(8,128)(2,1)S(1)}, u32[]{:S(2)}, u32[]{:S(2)}) collective-permute-start(bf16[2,128,128]{2,1,0:T(8,128)(2,1)S(1)} %pad_maximum_fusion), channel_id=1, source_target_pairs={{0,4},{4,8},{8,12},{12,16},{16,20},{20,24},{24,28},{1,5},{5,9},{9,... | collective-permute-start | bytes 196616 | tf_op jit(solution)/shard_map/ppermute | solution.py:26
  16.8 2.2 %slice-start = ((s8[5898240]{0:T(1024)(128)(4,1)}), s8[4194304]{0:T(1024)(128)(4,1)S(1)}, s32[]{:S(2)}) async-start(s8[5898240]{0:T(1024)(128)(4,1)} %bitcast.69), calls=%async_computation | async-start | bytes 8388608
  17.4 2.3 %slice-start.1 = ((s8[5898240]{0:T(1024)(128)(4,1)}), s8[1703936]{0:T(1024)(128)(4,1)S(1)}, s32[]{:S(2)}) async-start(s8[5898240]{0:T(1024)(128)(4,1)} %bitcast.69), calls=%async_computation.1 | async-start | bytes 3407872

commit v3 on v2

--- a/solution.py
+++ b/solution.py
@@ -197,17 +197,15 @@
     launch(0)
     for k in range(1, n_exp):
         links.send(own, everywhere.at[e, me], z_id + k, exp=piece_of(e, k))
-    for k in range(1, n_exp):
-        launch(k)
-        relay(k - 1)
-        if k > 1:
+    for k in range(1, n_exp + 3):
+        if k < n_exp:
+            launch(k)
+        if k - 1 < n_exp:
+            relay(k - 1)
+        if 0 <= k - 2 < n_exp:
             last(k - 2)
-    relay(n_exp - 1)
-    last(n_exp - 2)
-    finish(0)
-    last(n_exp - 1)
-    for k in range(1, n_exp):
-        finish(k)
+        if 0 <= k - 2 < n_exp:
+            finish(k - 2)
 
 
 def tile_of(size, most=256):
@@ -299,14 +297,14 @@
     n_seq,
     n_exp,
     hidden,
-    gate_col,
-    gate_row,
+    gates,
     weights,
     by_gate_in,
     by_up_in,
     mixed,
-    target,
+    control,
     grads_out,
+    gate_cols,
     factors,
     everywhere,
     part,
@@ -338,15 +336,22 @@
     greet(links, n_exp, False, 0)
     p_id, d_id, x_id, y_id, z_id = (links.new(n_exp) for _ in range(5))
     order = list(range(n_exp))[::-1]
+    gate_cols[...] = jnp.transpose(jnp.concatenate([gates[number] for number in range(n_seq)], axis=0))
+
+    def gate_col(piece):
+        rows = gate_cols[pl.ds(pl.multiple_of(piece * sub, sub), sub), :]
+        return jnp.concatenate([rows[:, number : number + 1] for number in range(n_seq)], axis=0)
+
 
     def produce(k):
         piece = piece_of(e, k)
+        gate = gate_col(piece)
         for start in range(0, width, 512):
             columns = slice(start, min(width, start + 512))
             outs = lax.dot_general(
                 hidden[piece], weights[:, columns], (((0,), (0,)), ((), ())), preferred_element_type=jnp.float32
             )
-            outs = (outs * gate_col[piece]).astype(jnp.bfloat16)
+            outs = (outs * gate).astype(jnp.bfloat16)
             part[k, :, :, :, columns] = outs.reshape(n_seq // 2, 2, sub, -1)
         links.send(part.at[k, :, 1 - core], pair.at[k], p_id + k, seq=C)
 
@@ -382,16 +387,14 @@
             links.send(from_x.at[k], landed.at[k - 1], z_id + k, exp=piece_of(e, k))
         return total
 
-    produce(order[0])
-    for before, k in zip(order, order[1:]):
-        produce(k)
-        merge(before)
-    merge(order[-1])
-    pass_on(order[0])
-    for before, k in zip(order, order[1:]):
-        pass_on(k)
-        collect(before)
-    total = collect(0) + mixed[...] - target[...]
+    stages = (produce, merge, pass_on, collect)
+    for now in range(n_exp + 3):
+        for lag, stage in enumerate(stages):
+            if 0 <= now - lag < n_exp and (lag < 3 or now - lag < n_exp - 1):
+                stage(order[now - lag])
+    steering = control[...]
+    target = STEER * steering / jnp.sqrt(jnp.sum(steering * steering, axis=-1, keepdims=True))
+    total = collect(0) + mixed[...] - target
     for k in order[:-1]:
         links.arrived(landed.at[k - 1], z_id + k)
         total = total + landed[k - 1].astype(jnp.float32)
@@ -401,11 +404,12 @@
 
     def consume(k):
         piece = piece_of(e, k)
+        gate = jnp.transpose(jnp.broadcast_to(gate_col(piece), (n_seq * sub, 128)))[0:1]
         lanes = pl.ds(pl.multiple_of(piece * (n_seq * sub), n_seq * sub), n_seq * sub)
 
         def step(index, carry):
             at = pl.ds(pl.multiple_of(index * tile, 16), tile)
-            d_hidden = times_rows(weights[at, :], everywhere[piece].reshape(-1, width)) * gate_row[piece]
+            d_hidden = times_rows(weights[at, :], everywhere[piece].reshape(-1, width)) * gate
             grads_out[0, at, lanes] = (d_hidden * factors[0, piece, at, :]).astype(jnp.bfloat16)
             grads_out[1, at, lanes] = (d_hidden * factors[1, piece, at, :]).astype(jnp.bfloat16)
             return carry
@@ -435,6 +439,7 @@
     route_gates = route_scores / jnp.sum(route_scores, axis=-1, keepdims=True)
     member = expert_ids[None, :, :] == jnp.arange(n_seq, dtype=jnp.int32)[:, None, None]
     gates = jnp.sum(jnp.where(member, route_gates[None], 0.0), axis=-1).reshape(n_seq, 1, seg_len)
+    vectors = jnp.stack([norm_gain, control])
     spread_count = 8 * n_exp
     ff = w_down.shape[1]
     group = n_seq * sub
@@ -462,15 +467,14 @@
         ],
         compiler_params=pltpu.CompilerParams(collective_id=0, has_side_effects=True),
         name="mix",
-    )(part, gates, norm_gain.reshape(1, width), jnp.swapaxes(w_gate_up[0], 1, 2))
-    gate_flat = gates_mine.reshape(n_seq, n_exp, sub).transpose(1, 0, 2).reshape(n_exp, group)
-    target = (STEER * control / jnp.sqrt(jnp.sum(control * control))).reshape(1, width)
+    )(part, gates, vectors[:1], jnp.swapaxes(w_gate_up[0], 1, 2))
     d_both = pl.pallas_call(
         functools.partial(error_kernel, n_seq, n_exp),
         out_shape=jax.ShapeDtypeStruct((2, ff, n_exp * group), bf16),
-        in_specs=[VM, VM, VM, VM, ANY, ANY, VM, VM],
+        in_specs=[VM, VM, VM, ANY, ANY, VM, VM],
         out_specs=VM,
         scratch_shapes=[
+            pltpu.VMEM((seg_len, n_seq), f32),
             pltpu.VMEM((2, n_exp, ff, group), f32),
             pltpu.VMEM((n_exp, n_seq, sub, width), bf16),
             pltpu.VMEM((n_exp, n_seq // 2, 2, sub, width), bf16),
@@ -486,7 +490,7 @@
         ],
         compiler_params=pltpu.CompilerParams(collective_id=1, has_side_effects=True),
         name="error",
-    )(hidden, gate_flat[:, :, None], gate_flat[:, None, :], w_down[0], by_gate, by_up, mixed, target)
+    )(hidden, gates_mine, w_down[0], by_gate, by_up, mixed, vectors[1:])
     grads = lax.dot_general(
         d_both.reshape(2 * ff, n_exp * group),
         rows.reshape(n_exp * group, width),

time: 209 us -> 196 us (0.938)
  Pallas kernels: 167 us -> 159 us
  other arithmetic: 8.24 us -> 4.88 us
    pallas_call x1, Pallas kernels: 92.1 us -> 88 us  [dense(): pl.pallas_call(functools.partial(error_kernel, n_seq, n_exp), out_shape=j...]
    pallas_call x1, Pallas kernels: 75.1 us -> 71.2 us  [dense(): pl.pallas_call(functools.partial(mix_kernel, n_seq, n_exp), out_shape=(ja...]
where the time goes in v3:
time: 196 us; the launch traced here: 195 us
  Pallas kernels  159 us (81%)
  matrix products  17.9 us (9%)
  local copies, waits for them, and re-layouts  10.2 us (5%)
  other arithmetic  4.88 us (2%)
  starting transfers between devices  2.39 us (1%)
    pallas_call x1, Pallas kernels, dense(): pl.pallas_call(functools.partial(error_kernel, n_seq, n_exp), out_shape=j...  88 us
    pallas_call x1, Pallas kernels, dense(): pl.pallas_call(functools.partial(mix_kernel, n_seq, n_exp), out_shape=(ja...  71.2 us
    dot_general x1, matrix products, dense(): lax.dot_general(d_both.reshape(2 * ff, n_exp * group), rows.reshape(n_exp...  14.9 us
    unnamed x7, local copies, waits for them, and re-layouts  4.43 us
  transfers between devices with their start and end apart: 1, of which 0 were waited for; matrix products, arithmetic and copies ran while one was open for 6% of the time, Pallas kernels for 0%

profile of v3, /device:TPU:0, one launch (start us, length us, event | category | flops | bytes accessed | tf_op | source)
XLA Modules:
  0.0 194.6 jit_solution(16737133077719817764)
XLA Ops:
  0.0 0.8 pad_maximum_fusion
  0.8 2.4 %collective-permute-start = (bf16[2,128,128]{2,1,0:T(8,128)(2,1)S(1)}, bf16[2,128,128]{2,1,0:T(8,128)(2,1)S(1)}, u32[]{:S(2)}, u32[]{:S(2)}) collective-permute-start(bf16[2,128,128]{2,1,0:T(8,128)(2,1)S(1)} %pad_maximum_fusion), channel_id=1, source_target_pairs={{0,4},{4,8},{8,12},{12,16},{16,20},{20,24},{24,28},{1,5},{5,9},{9,... | collective-permute-start | bytes 196616 | tf_op jit(solution)/shard_map/ppermute | solution.py:26
  3.2 0.9 copy.35
  4.0 0.9 copy.33
  5.0 0.7 max.18
  5.7 0.7 reduce_sum.28
  6.4 0.7 broadcast_divide_fusion
  7.1 1.3 stack.18.gain
  8.4 1.3 stack.19.control
  9.7 1.1 copy.36
  10.8 0.1 broadcast_in_dim.53
  11.0 1.0 constant_dynamic-update-slice_fusion
  11.9 0.8 compare_and_fusion
  12.7 1.3 select_reduce_fusion
  14.0 0.0 collective-permute-done
  14.0 0.1 copy.32
  14.1 0.1 copy.34
  14.2 0.5 fusion.1
  14.7 0.1 broadcast_maximum_fusion
  14.8 0.0 slice-start
  14.8 0.5 fusion.2
  15.3 0.1 exponential_add_fusion
  15.4 0.0 slice-start.1
  15.4 0.7 convolution_convert_fusion.1
  16.1 0.9 slice-done
  17.0 0.7 slice-done.1
  17.7 1.7 fusion
  19.4 1.2 copy.38
  20.6 71.2 %mix.1 = (bf16[4,8,32,2880]{3,2,1,0:T(8,128)(2,1)}, f32[32,2880]{1,0:T(8,128)}, f32[8,1,128]{2,1,0:T(1,128)}, bf16[4,720,256]{2,1,0:T(8,128)(2,1)}, f32[4,720,256]{2,1,0:T(8,128)}, /*index=5*/f32[4,720,256]{2,1,0:T(8,128)}) custom-call(bf16[4,32,2880]{2,1,0:T(8,128)(2,1)} %bitcast.53, f32[8,1,128]{2,1,0:T(1,128)} %bitcast.62, f32[1,2880]{1,0:T(1,128)} %stack.18.gain, ...), custom_call_target="tpu_custom_call" | custom-call | tf_op jit(solution)/shard_map/mix/pallas_call | solution.py:446
  91.7 88.0 %error.1 = bf16[2,720,1024]{2,1,0:T(8,128)(2,1)} custom-call(bf16[4,720,256]{2,1,0:T(8,128)(2,1)} %get-tuple-element.11.hidden, f32[8,1,128]{2,1,0:T(1,128)} %get-tuple-element.12.gates, bf16[720,2880]{1,0:T(8,128)(2,1)} %bitcast.52, f32[4,720,256]{2,1,0:T(8,128)} %get-tuple-element.13.by_gate_in, f32[4,720,256]{2,1,0:T(8,128)} %get-tuple-element.14.by_up_in, ...), custom_call_target="tpu_custom_call" | custom-call | tf_op jit(solution)/shard_map/error/pallas_call | solution.py:471
  179.7 14.9 %convolution_convert_fusion = bf16[1440,2880]{1,0:T(8,128)(2,1)} fusion(bf16[1440,1024]{1,0:T(8,128)(2,1)} %bitcast.54, bf16[1024,2880]{1,0:T(8,128)(2,1)} %bitcast.63), kind=kOutput, calls=%fused_computation | convolution fusion | flops 8497612800 | bytes 17141760 | tf_op jit(solution)/shard_map/dot_general | solution.py:494
  (4 shorter events, 0.0 us)
Async XLA Ops:
  0.8 13.2 %collective-permute-start = (bf16[2,128,128]{2,1,0:T(8,128)(2,1)S(1)}, bf16[2,128,128]{2,1,0:T(8,128)(2,1)S(1)}, u32[]{:S(2)}, u32[]{:S(2)}) collective-permute-start(bf16[2,128,128]{2,1,0:T(8,128)(2,1)S(1)} %pad_maximum_fusion), channel_id=1, source_target_pairs={{0,4},{4,8},{8,12},{12,16},{16,20},{20,24},{24,28},{1,5},{5,9},{9,... | collective-permute-start | bytes 196616 | tf_op jit(solution)/shard_map/ppermute | solution.py:26
  14.8 2.2 %slice-start = ((s8[5898240]{0:T(1024)(128)(4,1)}), s8[4194304]{0:T(1024)(128)(4,1)S(1)}, s32[]{:S(2)}) async-start(s8[5898240]{0:T(1024)(128)(4,1)} %bitcast.64), calls=%async_computation | async-start | bytes 8388608
  15.4 2.3 %slice-start.1 = ((s8[5898240]{0:T(1024)(128)(4,1)}), s8[1703936]{0:T(1024)(128)(4,1)S(1)}, s32[]{:S(2)}) async-start(s8[5898240]{0:T(1024)(128)(4,1)} %bitcast.64), calls=%async_computation.1 | async-start | bytes 3407872

commit v4 on v3

--- a/solution.py
+++ b/solution.py
@@ -220,7 +220,8 @@
     n_seq,
     n_exp,
     part,
-    gates,
+    expert_ids,
+    route_scores,
     gain,
     weights_in,
     rows_out,
@@ -229,6 +230,7 @@
     hidden_out,
     by_gate_out,
     by_up_out,
+    gates,
     weights,
     everywhere,
     landed,
@@ -246,6 +248,10 @@
     r_id, g_id = links.new(n_exp), links.new(n_seq)
     for k in range(1, n_exp):
         links.send(part.at[piece_of(e, k)], landed.at[k - 1], r_id + k, exp=piece_of(e, k))
+    route_gates = route_scores[...] / jnp.sum(route_scores[...], axis=0, keepdims=True)
+    for expert in range(n_seq):
+        member = expert_ids[...] == expert
+        gates[expert] = jnp.sum(jnp.where(member, route_gates, 0.0), axis=0, keepdims=True)
     for k in range(1, n_seq):
         peer = piece_of(me, k)
         links.send(gates.at[peer], gates_out.at[me], g_id + k, seq=peer)
@@ -436,9 +442,6 @@
     at = lax.axis_index("exp") * column_width
     placed = lax.dynamic_update_slice_in_dim(jnp.zeros((seg_len, width), bf16), residual, at, 1)
     part = (partial_value + placed.astype(f32)).astype(bf16).reshape(n_exp, sub, width)
-    route_gates = route_scores / jnp.sum(route_scores, axis=-1, keepdims=True)
-    member = expert_ids[None, :, :] == jnp.arange(n_seq, dtype=jnp.int32)[:, None, None]
-    gates = jnp.sum(jnp.where(member, route_gates[None], 0.0), axis=-1).reshape(n_seq, 1, seg_len)
     vectors = jnp.stack([norm_gain, control])
     spread_count = 8 * n_exp
     ff = w_down.shape[1]
@@ -453,9 +456,10 @@
             jax.ShapeDtypeStruct((n_exp, ff, group), f32),
             jax.ShapeDtypeStruct((n_exp, ff, group), f32),
         ),
-        in_specs=[VM, VM, VM, ANY],
+        in_specs=[VM, VM, VM, VM, ANY],
         out_specs=(ANY, VM, VM, VM, VM, VM),
         scratch_shapes=[
+            pltpu.VMEM((n_seq, 1, seg_len), f32),
             pltpu.VMEM((2, ff, width), bf16),
             pltpu.VMEM((n_exp, n_seq, sub, width), bf16),
             pltpu.VMEM((n_exp - 1, sub, width), bf16),
@@ -467,7 +471,7 @@
         ],
         compiler_params=pltpu.CompilerParams(collective_id=0, has_side_effects=True),
         name="mix",
-    )(part, gates, vectors[:1], jnp.swapaxes(w_gate_up[0], 1, 2))
+    )(part, expert_ids.T, route_scores.T, vectors[:1], jnp.swapaxes(w_gate_up[0], 1, 2))
     d_both = pl.pallas_call(
         functools.partial(error_kernel, n_seq, n_exp),
         out_shape=jax.ShapeDtypeStruct((2, ff, n_exp * group), bf16),

time: 196 us -> 193 us (0.985)
  other arithmetic: 4.88 us -> 2.22 us
    reduce_sum x2 -> x0, other arithmetic: 1.98 us -> none  [the longest x1 1.28 us: dense(): jnp.sum(jnp.where(member, route_gates[None], 0.0), axis=-1)]
  transfers between devices with their start and end apart: 1 -> 1, of which waited for: 0 -> 0; matrix products, arithmetic and copies ran while one was open for 6% -> 4% of each run, Pallas kernels for 0% -> 0%
where the time goes in v4:
time: 193 us; the launch traced here: 192 us
  Pallas kernels  159 us (82%)
  matrix products  17.9 us (9%)
  local copies, waits for them, and re-layouts  10.2 us (5%)
  starting transfers between devices  2.39 us (1%)
  other arithmetic  2.22 us (1%)
    pallas_call x1, Pallas kernels, dense(): pl.pallas_call(functools.partial(error_kernel, n_seq, n_exp), out_shape=j...  87.6 us
    pallas_call x1, Pallas kernels, dense(): pl.pallas_call(functools.partial(mix_kernel, n_seq, n_exp), out_shape=(ja...  71.2 us
    dot_general x1, matrix products, dense(): lax.dot_general(d_both.reshape(2 * ff, n_exp * group), rows.reshape(n_exp...  14.9 us
    unnamed x7, local copies, waits for them, and re-layouts  4.43 us
  transfers between devices with their start and end apart: 1, of which 0 were waited for; matrix products, arithmetic and copies ran while one was open for 4% of the time, Pallas kernels for 0%

profile of v4, /device:TPU:0, one launch (start us, length us, event | category | flops | bytes accessed | tf_op | source)
XLA Modules:
  0.0 191.7 jit_solution(18189763599908710478)
XLA Ops:
  0.0 0.8 pad_maximum_fusion
  0.8 2.4 %collective-permute-start = (bf16[2,128,128]{2,1,0:T(8,128)(2,1)S(1)}, bf16[2,128,128]{2,1,0:T(8,128)(2,1)S(1)}, u32[]{:S(2)}, u32[]{:S(2)}) collective-permute-start(bf16[2,128,128]{2,1,0:T(8,128)(2,1)S(1)} %pad_maximum_fusion), channel_id=1, source_target_pairs={{0,4},{4,8},{8,12},{12,16},{16,20},{20,24},{24,28},{1,5},{5,9},{9,... | collective-permute-start | bytes 196616 | tf_op jit(solution)/shard_map/ppermute | solution.py:26
  3.2 0.9 copy.24
  4.0 0.9 copy.22
  5.0 0.7 max.18
  5.7 1.3 stack.18.gain
  7.0 1.3 stack.19.control
  8.3 1.1 copy.25
  9.5 0.8 compare_and_fusion
  10.2 0.1 broadcast_in_dim.37
  10.3 1.0 constant_dynamic-update-slice_fusion
  11.3 0.0 collective-permute-done
  11.3 0.1 copy.21
  11.4 0.1 copy.23
  11.6 0.5 fusion.1
  12.1 0.1 broadcast_maximum_fusion
  12.1 0.0 slice-start
  12.1 0.5 fusion.2
  12.7 0.1 exponential_add_fusion
  12.7 0.0 slice-start.1
  12.7 0.7 convolution_convert_fusion.1
  13.4 0.9 slice-done
  14.3 0.7 slice-done.1
  15.0 1.7 fusion
  16.8 1.2 copy.27
  17.9 71.2 %mix.1 = (bf16[4,8,32,2880]{3,2,1,0:T(8,128)(2,1)}, f32[32,2880]{1,0:T(8,128)}, f32[8,1,128]{2,1,0:T(1,128)}, bf16[4,720,256]{2,1,0:T(8,128)(2,1)}, f32[4,720,256]{2,1,0:T(8,128)}, /*index=5*/f32[4,720,256]{2,1,0:T(8,128)}) custom-call(bf16[4,32,2880]{2,1,0:T(8,128)(2,1)} %bitcast.54, s32[4,128]{1,0:T(4,128)} %bitcast.63, f32[4,128]{1,0:T(4,128)} %bitcast.64, ...), custom_call_target="tpu_custom_call" | custom-call | tf_op jit(solution)/shard_map/mix/pallas_call | solution.py:449
  89.1 87.6 %error.1 = bf16[2,720,1024]{2,1,0:T(8,128)(2,1)} custom-call(bf16[4,720,256]{2,1,0:T(8,128)(2,1)} %get-tuple-element.11.hidden, f32[8,1,128]{2,1,0:T(1,128)} %get-tuple-element.12.gates, bf16[720,2880]{1,0:T(8,128)(2,1)} %bitcast.53, f32[4,720,256]{2,1,0:T(8,128)} %get-tuple-element.13.by_gate_in, f32[4,720,256]{2,1,0:T(8,128)} %get-tuple-element.14.by_up_in, ...), custom_call_target="tpu_custom_call" | custom-call | tf_op jit(solution)/shard_map/error/pallas_call | solution.py:475
  176.7 14.9 %convolution_convert_fusion = bf16[1440,2880]{1,0:T(8,128)(2,1)} fusion(bf16[1440,1024]{1,0:T(8,128)(2,1)} %bitcast.55, bf16[1024,2880]{1,0:T(8,128)(2,1)} %bitcast.65), kind=kOutput, calls=%fused_computation | convolution fusion | flops 8497612800 | bytes 17141760 | tf_op jit(solution)/shard_map/dot_general | solution.py:498
  (4 shorter events, 0.0 us)
Async XLA Ops:
  0.8 10.5 %collective-permute-start = (bf16[2,128,128]{2,1,0:T(8,128)(2,1)S(1)}, bf16[2,128,128]{2,1,0:T(8,128)(2,1)S(1)}, u32[]{:S(2)}, u32[]{:S(2)}) collective-permute-start(bf16[2,128,128]{2,1,0:T(8,128)(2,1)S(1)} %pad_maximum_fusion), channel_id=1, source_target_pairs={{0,4},{4,8},{8,12},{12,16},{16,20},{20,24},{24,28},{1,5},{5,9},{9,... | collective-permute-start | bytes 196616 | tf_op jit(solution)/shard_map/ppermute | solution.py:26
  12.1 2.2 %slice-start = ((s8[5898240]{0:T(1024)(128)(4,1)}), s8[4194304]{0:T(1024)(128)(4,1)S(1)}, s32[]{:S(2)}) async-start(s8[5898240]{0:T(1024)(128)(4,1)} %bitcast.66), calls=%async_computation | async-start | bytes 8388608
  12.7 2.3 %slice-start.1 = ((s8[5898240]{0:T(1024)(128)(4,1)}), s8[1703936]{0:T(1024)(128)(4,1)S(1)}, s32[]{:S(2)}) async-start(s8[5898240]{0:T(1024)(128)(4,1)} %bitcast.66), calls=%async_computation.1 | async-start | bytes 3407872
